TPU v7x, 32 devices: a whole 2x2x4 slice. The times are simulated.
32 devices in a mesh: shot: 4 (over z), tile: 8 (over y, x, core).
Axes of the slice: x: 2, y: 2, z: 4, core: 2. Of those that a mesh axis runs over, the one named last changes fastest.
Arguments:
- traces: bfloat16 [2, 4, 1024, 2048], P(None, 'shot', 'tile'), may hold values from -6 to 6
- start: int32 [4, 8, 8], P('shot'), may hold values from 0 to 1536
- depth_index: int32 [4, 8, 8, 256], P('shot', 'tile'), may hold values from 0 to 510
- depth_frac: bfloat16 [4, 8, 8, 256], P('shot', 'tile'), may hold values from 0 to 1
- aperture: int32 [4, 8, 4], P('shot'), may hold values from -1 to 7, as said below
- amplitude: bfloat16 [4, 8, 8, 384, 128], P('shot', 'tile'), may hold values from -0.5 to 0.5
Outputs:
- migrated: float32 [3072, 256], P('tile', 'shot')
Inputs may be any that keep to these rules, and one draw needn't show every extreme that they name: `aperture`: each list holds 1 to 4 block ids, ascending and consecutive, then -1 in the remaining slots; in every shot some tile's list is full.
All inputs are finite; a program needn't handle non-finite values.
Results may differ from a plain program's by a relative error of at most 0.0041.
Values may be sent and summed in bfloat16 or wider, within the bound.
No kernel may reach another device: no remote copies, remote signals or barrier semaphores. Data moves between devices by JAX's collectives and lax.ppermute only.
A program may use at most 64 MiB of HBM per device.

v0:
```python
import jax
import jax.numpy as jnp
from jax import lax
from jax.sharding import PartitionSpec as P

TW = 512


def depth_group(window_group, rows_group, fraction_group):
    width = window_group.shape[3]
    depth = rows_group.shape[1]
    sample_pos = jnp.arange(width, dtype=jnp.int32)[None, :, None]
    lower_hot = (sample_pos == rows_group[:, None, :]).astype(jnp.bfloat16)
    upper_hot = (sample_pos == rows_group[:, None, :] + 1).astype(jnp.bfloat16)
    both_hot = jnp.concatenate([lower_hot, upper_hot], axis=2)
    picked = jnp.einsum(
        "bprt,btz->bprz", window_group, both_hot, preferred_element_type=jnp.float32
    )
    lower_sample = picked[..., :depth]
    upper_sample = picked[..., depth:]
    weight = fraction_group.astype(jnp.float32)[:, None, None, :]
    return ((1.0 - weight) * lower_sample + weight * upper_sample).astype(jnp.bfloat16)


def to_depth_blocks(windows, sample_rows, fraction):
    blocks = windows.shape[0]
    groups = blocks // 8
    per_group = blocks // groups

    def one_group(items):
        return depth_group(items[0], items[1], items[2])

    grouped = (
        windows.reshape((groups, per_group) + windows.shape[1:]),
        sample_rows.reshape((groups, per_group) + sample_rows.shape[1:]),
        fraction.reshape((groups, per_group) + fraction.shape[1:]),
    )
    result = lax.map(one_group, grouped)
    return result.reshape((blocks,) + result.shape[2:])


def local(traces, start, depth_index, depth_frac, aperture, amplitude):
    my_tile = lax.axis_index("tile")
    my_gather = traces[:, 0]
    aperture_rows = aperture[0]
    tile_count = aperture_rows.shape[0]
    wanted = jnp.any(aperture_rows == my_tile, axis=1)
    my_starts = lax.dynamic_index_in_dim(start[0], my_tile, axis=1, keepdims=False)

    def cut_window(block_pos, filled):
        first_sample = my_starts[block_pos]
        piece = lax.dynamic_slice_in_dim(my_gather, first_sample, TW, 2)
        return lax.dynamic_update_index_in_dim(filled, piece, block_pos, 0)

    empty = jnp.zeros((tile_count,) + my_gather.shape[:2] + (TW,), jnp.bfloat16)
    windows = lax.fori_loop(0, tile_count, cut_window, empty)
    windows = jnp.where(wanted[:, None, None, None], windows, jnp.zeros_like(windows))
    received = lax.all_to_all(windows, "tile", split_axis=0, concat_axis=0, tiled=True)
    depth_traces = to_depth_blocks(received, depth_index[0, 0], depth_frac[0, 0])
    weights = amplitude[0, 0]
    partial_value = jnp.einsum(
        "bcr,bprz->pcz", weights, depth_traces, preferred_element_type=jnp.float32
    )
    magnitude = jnp.sqrt(partial_value[0] ** 2 + partial_value[1] ** 2)
    inverse = 1.0 / jnp.maximum(magnitude, 1.0)
    summed = (
        lax.psum_scatter(partial_value[0], "shot", scatter_dimension=1, tiled=True),
        lax.psum_scatter(partial_value[0] * inverse, "shot", scatter_dimension=1, tiled=True),
        lax.psum_scatter(partial_value[1] * inverse, "shot", scatter_dimension=1, tiled=True),
    )
    shot_count = lax.axis_size("shot")
    return summed[0] * (summed[1] ** 2 + summed[2] ** 2) / (shot_count * shot_count)


def solution(mesh):
    in_specs = (
        P(None, "shot", "tile", None),
        P("shot", None, None),
        P("shot", "tile", None, None),
        P("shot", "tile", None, None),
        P("shot", None, None),
        P("shot", "tile", None, None, None),
    )
    out_specs = P("tile", "shot")
    return jax.shard_map(local, mesh=mesh, in_specs=in_specs, out_specs=out_specs, check_vma=False)
```

profile of v0, /device:TPU:0, one launch (start us, length us, event | category | flops | bytes accessed | tf_op | source)
XLA Modules:
  0.0 145.2 jit_solution(13419167691825609606)
XLA Ops:
  6.5 0.0 copy-start
  6.5 0.0 copy-start.3
  6.5 1.0 dynamic-slice_reduce_fusion
  7.5 28.7 %while.18 = (s32[]{:T(128)}, bf16[8,2,128,512]{3,2,1,0:T(8,128)(2,1)S(1)}, s32[8]{0:T(128)S(1)}, bf16[2,128,2048]{2,1,0:T(8,128)(2,1)}) while((s32[]{:T(128)}, bf16[8,2,128,512]{3,2,1,0:T(8,128)(2,1)S(1)}, s32[8]{0:T(128)S(1)}, bf16[2,128,2048]{2,1,0:T(8,128)(2,1)}) %tuple.44), condition=%wide.region_2.3_spmd.clone, body=%wide.region_1.2_spmd.sunk.clone | while | flops 5 | bytes 524395 | solution.py:56
  7.5 0.6 dynamic_slice.35
  9.9 1.1 bitcast_dynamic-update-slice_fusion.3
  11.1 0.6 dynamic_slice.35
  13.5 1.1 bitcast_dynamic-update-slice_fusion.3
  14.7 0.6 dynamic_slice.35
  17.1 1.1 bitcast_dynamic-update-slice_fusion.3
  18.3 0.6 dynamic_slice.35
  20.7 1.1 bitcast_dynamic-update-slice_fusion.3
  21.9 0.6 dynamic_slice.35
  24.3 1.1 bitcast_dynamic-update-slice_fusion.3
  25.4 0.6 dynamic_slice.35
  27.9 1.1 bitcast_dynamic-update-slice_fusion.3
  29.0 0.6 dynamic_slice.35
  31.5 1.1 bitcast_dynamic-update-slice_fusion.3
  32.6 0.6 dynamic_slice.35
  35.1 1.1 bitcast_dynamic-update-slice_fusion.3
  36.2 0.0 copy-done.3
  36.2 1.5 %broadcast_select_fusion = bf16[8,2,128,512]{3,2,1,0:T(8,128)(2,1)} fusion(bf16[8,2,128,512]{3,2,1,0:T(8,128)(2,1)S(1)} %get-tuple-element.99, pred[8]{0:T(512)(128)(4,1)S(1)} %compare_reduce_fusion), kind=kLoop, calls=%fused_computation.11 | loop fusion | flops 1048576 | bytes 4194312 | tf_op jit(solution)/shard_map/jit(_where)/select_n | solution.py:57
  37.8 0.0 copy-start.2
  37.8 0.0 copy-start.1
  37.8 5.3 %all-to-all-start = ((bf16[8,2,128,512]{3,2,1,0:T(8,128)(2,1)}), bf16[8,2,128,512]{3,2,1,0:T(8,128)(2,1)S(1)}, u32[]{:S(2)}, u32[]{:S(2)}) async-start(bf16[8,2,128,512]{3,2,1,0:T(8,128)(2,1)} %broadcast_select_fusion), calls=%async_computation | async-start | bytes 4194304 | tf_op jit(solution)/shard_map/all_to_all | solution.py:58
  43.1 0.0 reduce-scatter.6.cloned.1.call-start
  43.1 0.0 copy-done.2
  43.2 0.0 copy-done.1
  43.2 2.6 %iota_compare_fusion = (pred[8,512,256]{2,1,0:T(32,128)(4,1)}, pred[8,512,256]{2,1,0:T(32,128)(4,1)}) fusion(s32[8,256]{1,0:T(8,128)S(1)} %broadcast_add_fusion, s32[8,256]{1,0:T(8,128)S(1)} %bitcast.47), kind=kLoop, calls=%fused_computation.5 | loop fusion | flops 2097152 | bytes 2113536 | tf_op jit(solution)/shard_map/while/body/eval_jaxpr/eq | solution.py:14
  45.8 24.0 %all-to-all-done = bf16[8,2,128,512]{3,2,1,0:T(8,128)(2,1)S(1)} async-done(((bf16[8,2,128,512]{3,2,1,0:T(8,128)(2,1)}), bf16[8,2,128,512]{3,2,1,0:T(8,128)(2,1)S(1)}, u32[]{:S(2)}, u32[]{:S(2)}) %all-to-all-start) | async-done | bytes 2097184 | tf_op jit(solution)/shard_map/all_to_all | solution.py:58
  69.7 2.8 %fusion = f32[8,2,128,512]{3,2,1,0:T(8,128)S(1)} fusion(bf16[8,2,128,512]{3,2,1,0:T(8,128)(2,1)S(1)} %all-to-all-done, pred[8,512,256]{2,1,0:T(32,128)(4,1)} %get-tuple-element.110, pred[8,512,256]{2,1,0:T(32,128)(4,1)} %get-tuple-element.111), kind=kOutput, calls=%fused_computation.2 | convolution fusion | flops 1075838976 | bytes 8388608 | tf_op jit(solution)/shard_map/while/body/eval_jaxpr/bprt,btz->bprz/dot_general | solution.py:16
  72.6 0.0 copy-done
  72.6 0.8 convolution_bitcast_fusion
  73.4 1.1 fusion.10
  74.5 0.0 reduce-scatter.6.cloned.1.call-update
  74.5 0.0 reduce-scatter.8.cloned.1.call-start
  74.5 0.7 reduce-scatter.8.cloned.1.call-update
  75.2 0.0 reduce-scatter.4.cloned.1.call-start
  75.3 0.8 slice_bitcast_fusion.1
  76.0 0.0 reduce-scatter.4.cloned.1.call-update
  76.1 18.6 %reduce-scatter.6.cloned.1.call-done = f32[384,64]{0,1:T(8,128)} async-done(((f32[384,256]{0,1:T(8,128)}), f32[384,64]{0,1:T(8,128)}) %reduce-scatter.6.cloned.1.call-update) | async-done | bytes 98320 | tf_op jit(solution)/shard_map/reduce_scatter | solution.py:68
  94.6 21.2 %reduce-scatter.8.cloned.1.call-done = f32[384,64]{0,1:T(8,128)} async-done(((f32[384,256]{0,1:T(8,128)}), f32[384,64]{0,1:T(8,128)}) %reduce-scatter.8.cloned.1.call-update) | async-done | bytes 98320 | tf_op jit(solution)/shard_map/reduce_scatter | solution.py:69
  115.9 21.2 %reduce-scatter.4.cloned.1.call-done = f32[384,64]{0,1:T(8,128)} async-done(((f32[384,256]{0,1:T(8,128)}), f32[384,64]{0,1:T(8,128)}) %reduce-scatter.4.cloned.1.call-update) | async-done | bytes 98320 | tf_op jit(solution)/shard_map/reduce_scatter | solution.py:67
  137.0 1.6 %multiply_multiply_fusion = f32[384,64]{0,1:T(8,128)} fusion(f32[384,64]{0,1:T(8,128)} %reduce-scatter.4.cloned.1.call-done, f32[384,64]{0,1:T(8,128)} %reduce-scatter.8.cloned.1.call-done, f32[384,64]{0,1:T(8,128)} %reduce-scatter.6.cloned.1.call-done), kind=kLoop, calls=%fused_computation.21 | loop fusion | flops 122880 | bytes 393216 | tf_op jit(solution)/shard_map/div | solution.py:72
  (5 shorter events, 0.0 us)
Async XLA Ops:
  6.5 66.0 %copy-start = (bf16[1,1,8,384,128]{4,3,2,1,0:T(8,128)(2,1)S(1)}, bf16[1,1,8,384,128]{4,3,2,1,0:T(8,128)(2,1)}, u32[]{:S(2)}) copy-start(bf16[1,1,8,384,128]{4,3,2,1,0:T(8,128)(2,1)} %param.13) | copy-start | bytes 2359300
  6.5 29.7 %copy-start.3 = (s32[1,8,4]{1,2,0:T(4,128)S(1)}, s32[1,8,4]{1,2,0:T(4,128)}, u32[]{:S(2)}) copy-start(s32[1,8,4]{1,2,0:T(4,128)} %param.12) | copy-start | bytes 388
  37.8 5.4 %copy-start.2 = (bf16[1,1,8,256]{3,2,1,0:T(8,128)(2,1)S(1)}, bf16[1,1,8,256]{3,2,1,0:T(8,128)(2,1)}, u32[]{:S(2)}) copy-start(bf16[1,1,8,256]{3,2,1,0:T(8,128)(2,1)} %param.11) | copy-start | bytes 12292
  37.8 5.4 %copy-start.1 = (s32[1,1,8,256]{3,2,1,0:T(8,128)S(1)}, s32[1,1,8,256]{3,2,1,0:T(8,128)}, u32[]{:S(2)}) copy-start(s32[1,1,8,256]{3,2,1,0:T(8,128)} %param.10) | copy-start | bytes 24580
  37.8 31.9 %all-to-all-start = ((bf16[8,2,128,512]{3,2,1,0:T(8,128)(2,1)}), bf16[8,2,128,512]{3,2,1,0:T(8,128)(2,1)S(1)}, u32[]{:S(2)}, u32[]{:S(2)}) async-start(bf16[8,2,128,512]{3,2,1,0:T(8,128)(2,1)} %broadcast_select_fusion), calls=%async_computation | async-start | bytes 4194304 | tf_op jit(solution)/shard_map/all_to_all | solution.py:58
  43.1 51.5 %reduce-scatter.6.cloned.1.call-start = ((), (), s32[]{:S(2)}) async-start(), calls=%async_computation.5 | async-start | bytes 491520 | tf_op jit(solution)/shard_map/reduce_scatter | solution.py:68
  74.5 41.4 %reduce-scatter.8.cloned.1.call-start = ((), (), s32[]{:S(2)}) async-start(), calls=%async_computation.6 | async-start | bytes 491520 | tf_op jit(solution)/shard_map/reduce_scatter | solution.py:69
  75.2 61.8 %reduce-scatter.4.cloned.1.call-start = ((), (), s32[]{:S(2)}) async-start(), calls=%async_computation.4 | async-start | bytes 491520 | tf_op jit(solution)/shard_map/reduce_scatter | solution.py:67
Sparse Core Ops, SparseCore 0:
  74.6 19.9 reduce-scatter.5
  97.0 18.8 reduce-scatter.7
  118.2 18.8 reduce-scatter.3
where the time goes:
time: 146 us; the launch traced here: 145 us
  waiting for transfers between devices  85.7 us (59%)
  local copies, waits for them, and re-layouts  15.7 us (11%)
  loops' own time  14.8 us (10%)
  between operations  13.2 us (9%)
  other arithmetic  6.88 us (5%)
  starting transfers between devices  5.42 us (4%)
  matrix products  3.61 us (2%)
    all_to_all x1, waiting for transfers between devices, local(): lax.all_to_all(windows, 'tile', split_axis=0, concat_axis=0, tiled=True)  24 us
    reduce_scatter x1, waiting for transfers between devices, local(): lax.psum_scatter(partial_value[1] * inverse, 'shot', scatter_dimension=1,...  21.2 us
    reduce_scatter x1, waiting for transfers between devices, local(): lax.psum_scatter(partial_value[0], 'shot', scatter_dimension=1, tiled=True)  21.2 us
    reduce_scatter x1, waiting for transfers between devices, local(): lax.psum_scatter(partial_value[0] * inverse, 'shot', scatter_dimension=1,...  18.6 us
    another operation x1, loops' own time, local(): windows = lax.fori_loop(0, tile_count, cut_window, empty)  14.8 us
    dynamic_update_slice x8, local copies, waits for them, and re-layouts, cut_window(): return lax.dynamic_update_index_in_dim(filled, piece, block_pos, 0)  8.98 us
    all_to_all x1, starting transfers between devices, local(): lax.all_to_all(windows, 'tile', split_axis=0, concat_axis=0, tiled=True)  5.3 us
    dynamic_slice x8, local copies, waits for them, and re-layouts, cut_window(): first_sample = my_starts[block_pos]  4.93 us
  transfers between devices with their start and end apart: 4, of which 4 were waited for; matrix products, arithmetic and copies ran while one was open for 2% of the time, Pallas kernels for 0%

commit v1 on v0

v1 whole, which is shorter than its diff:
```python
import functools

import jax
import jax.numpy as jnp
from jax import lax
from jax.experimental import pallas as pl
from jax.experimental.pallas import tpu as pltpu
from jax.sharding import PartitionSpec as P

TW = 512
LANES = 128
SLAB = TW + LANES
NT_DIMS = (((1,), (1,)), ((), ()))


def partner(pos, step, count):
    if count & (count - 1) == 0:
        return pos ^ step
    return (pos + step) % count


def source_of(pos, step, count):
    if count & (count - 1) == 0:
        return pos ^ step
    return (pos - step + count) % count


def pairs(step, count):
    return [(pos, partner(pos, step, count)) for pos in range(count)]


def depth_kernel(tiles, start_ref, aperture_ref, rows_ref, frac_ref, traces_ref, *out_refs):
    me = lax.axis_index("tile")
    samples = traces_ref.shape[2]
    depth = rows_ref.shape[1]
    rows_columns = rows_ref[...].T
    frac_columns = frac_ref[...].T
    column = lax.broadcasted_iota(jnp.int32, rows_columns.shape, 1)
    lane = lax.broadcasted_iota(jnp.int32, (depth, SLAB), 1).astype(jnp.float32)
    for step in range(tiles):
        tile = partner(me, step, tiles)
        listed = aperture_ref[tile, 0] == me
        for slot in range(1, aperture_ref.shape[1]):
            listed = jnp.logical_or(listed, aperture_ref[tile, slot] == me)
        out_ref = out_refs[step]

        @pl.when(listed)
        def _():
            first = start_ref[tile, me]
            slab = jnp.minimum(first // LANES, (samples - SLAB) // LANES) * LANES
            slab = pl.multiple_of(slab, LANES)
            mine = column == tile
            row = jnp.sum(jnp.where(mine, rows_columns, 0.0), axis=1, keepdims=True)
            weight = jnp.sum(jnp.where(mine, frac_columns, 0.0), axis=1, keepdims=True)
            row = row + (first - slab).astype(jnp.float32)
            lower_hot = (lane == row).astype(jnp.bfloat16)
            upper_hot = (lane == row + 1.0).astype(jnp.bfloat16)
            window = jnp.concatenate(
                [traces_ref[0, :, pl.ds(slab, SLAB)], traces_ref[1, :, pl.ds(slab, SLAB)]], axis=0
            )
            lower = lax.dot_general(lower_hot, window, NT_DIMS, preferred_element_type=jnp.float32)
            upper = lax.dot_general(upper_hot, window, NT_DIMS, preferred_element_type=jnp.float32)
            out_ref[...] = ((1.0 - weight) * lower + weight * upper).astype(jnp.bfloat16)

        @pl.when(jnp.logical_not(listed))
        def _():
            out_ref[...] = jnp.zeros_like(out_ref)


def partial_kernel(tiles, shots, amplitude_ref, *refs):
    me = lax.axis_index("tile")
    my_shot = lax.axis_index("shot")
    depth_refs = refs[:tiles]
    own_ref, out_refs, total_ref = refs[tiles], refs[tiles + 1 : -1], refs[-1]
    receivers = amplitude_ref.shape[2]
    piece = own_ref.shape[1]
    group = 8
    for base in range(0, tiles, group):
        steps = range(base, min(base + group, tiles))
        weights = jnp.concatenate(
            [amplitude_ref[source_of(me, step, tiles)] for step in steps], axis=1
        )
        for part in range(2):
            traces = jnp.concatenate(
                [
                    depth_refs[step][:, part * receivers : (part + 1) * receivers]
                    for step in steps
                ],
                axis=1,
            )
            added = lax.dot_general(traces, weights, NT_DIMS, preferred_element_type=jnp.float32)
            if base:
                added = added + total_ref[part]
            total_ref[part] = added
    for part in range(2):
        own_ref[part] = total_ref[part, pl.ds(pl.multiple_of(my_shot * piece, piece), piece), :]
        for step in range(1, shots):
            target = partner(my_shot, step, shots)
            rows = pl.ds(pl.multiple_of(target * piece, piece), piece)
            out_refs[step - 1][part] = total_ref[part, rows, :].astype(jnp.bfloat16)


def image_kernel(shots, *refs):
    out_ref = refs[-1]
    stack = None
    for ref in refs[:shots]:
        real = ref[0].astype(jnp.float32)
        imag = ref[1].astype(jnp.float32)
        inverse = 1.0 / jnp.maximum(jnp.sqrt(real * real + imag * imag), 1.0)
        if stack is None:
            stack, first, second = real, real * inverse, imag * inverse
        else:
            stack = stack + real
            first = first + real * inverse
            second = second + imag * inverse
    out_ref[...] = stack * (first * first + second * second) / (shots * shots)


VMEM = pl.BlockSpec(memory_space=pltpu.VMEM)
SMEM = pl.BlockSpec(memory_space=pltpu.SMEM)


def local(traces, start, depth_index, depth_frac, aperture, amplitude):
    tiles = lax.axis_size("tile")
    shots = lax.axis_size("shot")
    parts, _, receivers, samples = traces.shape
    depth = depth_index.shape[3]
    columns = amplitude.shape[3]
    piece = depth // shots

    wanted = jnp.stack(
        [depth_index[0, 0].astype(jnp.float32), depth_frac[0, 0].astype(jnp.float32)], axis=1
    )
    wanted = lax.all_to_all(wanted, "tile", split_axis=0, concat_axis=0, tiled=True)

    block = jax.ShapeDtypeStruct((depth, parts * receivers), jnp.bfloat16)
    sent = pl.pallas_call(
        functools.partial(depth_kernel, tiles),
        out_shape=[block] * tiles,
        in_specs=[SMEM, SMEM, VMEM, VMEM, VMEM],
        out_specs=[VMEM] * tiles,
        compiler_params=pltpu.CompilerParams(vmem_limit_bytes=32 << 20),
    )(start[0], aperture[0], wanted[:, 0], wanted[:, 1], traces[:, 0])
    received = [sent[0]]
    for step in range(1, tiles):
        received.append(lax.ppermute(sent[step], "tile", pairs(step, tiles)))

    own = jax.ShapeDtypeStruct((parts, piece, columns), jnp.float32)
    other = jax.ShapeDtypeStruct((parts, piece, columns), jnp.bfloat16)
    pieces = pl.pallas_call(
        functools.partial(partial_kernel, tiles, shots),
        out_shape=[own] + [other] * (shots - 1),
        in_specs=[VMEM] * (1 + tiles),
        out_specs=[VMEM] * shots,
        scratch_shapes=[pltpu.VMEM((parts, depth, columns), jnp.float32)],
        compiler_params=pltpu.CompilerParams(vmem_limit_bytes=32 << 20),
    )(amplitude[0, 0], *received)
    summed = [pieces[0]]
    for step in range(1, shots):
        summed.append(lax.ppermute(pieces[step], "shot", pairs(step, shots)))

    image = pl.pallas_call(
        functools.partial(image_kernel, shots),
        out_shape=jax.ShapeDtypeStruct((piece, columns), jnp.float32),
        in_specs=[VMEM] * shots,
        out_specs=VMEM,
    )(*summed)
    return image.T


def solution(mesh):
    in_specs = (
        P(None, "shot", "tile", None),
        P("shot", None, None),
        P("shot", "tile", None, None),
        P("shot", "tile", None, None),
        P("shot", None, None),
        P("shot", "tile", None, None, None),
    )
    out_specs = P("tile", "shot")
    return jax.shard_map(local, mesh=mesh, in_specs=in_specs, out_specs=out_specs, check_vma=False)
```

time: 146 us -> 49.2 us (0.34)
  waiting for transfers between devices: 85.7 us -> 22.6 us
  loops' own time: 14.8 us -> 0 us
  between operations: 13.2 us -> 0.08 us
  local copies, waits for them, and re-layouts: 15.7 us -> 4.04 us
  starting transfers between devices: 5.42 us -> 16.1 us
  other arithmetic: 6.88 us -> 1.33 us
  Pallas kernels: 0 us -> 5 us
  matrix products: 3.61 us -> 0 us
    reduce_scatter x3 -> x0, waiting for transfers between devices: 61 us -> none  [the longest x1 21.2 us: local(): lax.psum_scatter(partial_value[1] * inverse, 'shot', scatter_dimension=1,...]
    all_to_all x1, waiting for transfers between devices: 24 us -> 4.67 us  [local(): lax.all_to_all(wanted, 'tile', split_axis=0, concat_axis=0, tiled=True)]
    ppermute x0 -> x10, waiting for transfers between devices: none -> 17.9 us  [the longest x7 9.6 us: local(): received.append(lax.ppermute(sent[step], 'tile', pairs(step, tiles)))]
    another operation x1 -> x0, loops' own time: 14.8 us -> none  [local(): windows = lax.fori_loop(0, tile_count, cut_window, empty)]
    ppermute x0 -> x10, starting transfers between devices: none -> 10.8 us  [the longest x7 5.46 us: local(): received.append(lax.ppermute(sent[step], 'tile', pairs(step, tiles)))]
    dynamic_update_slice x8 -> x0, local copies, waits for them, and re-layouts: 8.98 us -> none  [cut_window(): return lax.dynamic_update_index_in_dim(filled, piece, block_pos, 0)]
    dynamic_slice x9 -> x0, local copies, waits for them, and re-layouts: 5.89 us -> none  [the longest x8 4.93 us: cut_window(): first_sample = my_starts[block_pos]]
    pallas_call x0 -> x3, Pallas kernels: none -> 5 us  [the longest x1 2.25 us: local(): pl.pallas_call(functools.partial(depth_kernel, tiles), out_shape=[block]...]
  transfers between devices with their start and end apart: 4 -> 11, of which waited for: 4 -> 6; matrix products, arithmetic and copies ran while one was open for 2% -> 0% of each run, Pallas kernels for 0% -> 0%
where the time goes in v1:
time: 49.2 us; the launch traced here: 49.1 us
  waiting for transfers between devices  22.6 us (46%)
  starting transfers between devices  16.1 us (33%)
  Pallas kernels  5 us (10%)
  local copies, waits for them, and re-layouts  4.04 us (8%)
  other arithmetic  1.33 us (3%)
    ppermute x7, waiting for transfers between devices, local(): received.append(lax.ppermute(sent[step], 'tile', pairs(step, tiles)))  9.6 us
    ppermute x3, waiting for transfers between devices, local(): summed.append(lax.ppermute(pieces[step], 'shot', pairs(step, shots)))  8.29 us
    ppermute x7, starting transfers between devices, local(): received.append(lax.ppermute(sent[step], 'tile', pairs(step, tiles)))  5.46 us
    all_to_all x1, starting transfers between devices, local(): lax.all_to_all(wanted, 'tile', split_axis=0, concat_axis=0, tiled=True)  5.3 us
    ppermute x3, starting transfers between devices, local(): summed.append(lax.ppermute(pieces[step], 'shot', pairs(step, shots)))  5.3 us
    all_to_all x1, waiting for transfers between devices, local(): lax.all_to_all(wanted, 'tile', split_axis=0, concat_axis=0, tiled=True)  4.67 us
    unnamed x19, local copies, waits for them, and re-layouts  3.94 us
    pallas_call x1, Pallas kernels, local(): pl.pallas_call(functools.partial(depth_kernel, tiles), out_shape=[block]...  2.25 us
  transfers between devices with their start and end apart: 11, of which 6 were waited for; matrix products, arithmetic and copies ran while one was open for 0% of the time, Pallas kernels for 0%

profile of v1, /device:TPU:0, one launch (start us, length us, event | category | flops | bytes accessed | tf_op | source)
XLA Modules:
  0.0 49.1 jit_solution(1937361955697159925)
XLA Ops:
  0.0 0.7 %convert_element_type.31 = f32[1,1,8,256]{3,2,1,0:T(8,128)S(1)} convert(s32[1,1,8,256]{3,2,1,0:T(8,128)} %param.8) | non-fusion elementwise | flops 2048 | bytes 16384 | tf_op jit(solution)/shard_map/convert_element_type | solution.py:132
  0.7 0.0 copy-start.7
  0.7 0.7 %copy-done.7 = bf16[1,1,8,256]{3,2,1,0:T(8,128)(2,1)S(1)} copy-done((bf16[1,1,8,256]{3,2,1,0:T(8,128)(2,1)S(1)}, bf16[1,1,8,256]{3,2,1,0:T(8,128)(2,1)}, u32[]{:S(2)}) %copy-start.7) | copy-done | bytes 4120
  1.4 0.6 %pad_maximum_fusion = f32[8,2,256]{2,1,0:T(2,128)} fusion(f32[8,1,256]{2,1,0:T(1,128)S(1)} %bitcast_convert_fusion, f32[8,1,256]{2,1,0:T(1,128)S(1)} %bitcast.18), kind=kLoop, calls=%fused_computation | loop fusion | flops 4096 | bytes 32768 | tf_op jit(solution)/shard_map/stack | solution.py:131
  2.0 0.0 copy-start.8
  2.0 5.3 %all-to-all-start = ((f32[8,2,256]{2,1,0:T(2,128)}), f32[8,2,256]{2,1,0:T(2,128)S(1)}, u32[]{:S(2)}, u32[]{:S(2)}) async-start(f32[8,2,256]{2,1,0:T(2,128)} %pad_maximum_fusion), calls=%async_computation | async-start | bytes 32768 | tf_op jit(solution)/shard_map/all_to_all | solution.py:134
  7.3 0.0 copy-done.8
  7.3 0.1 copy.12.aperture_ref
  7.4 4.7 %all-to-all-done = f32[8,2,256]{2,1,0:T(2,128)S(1)} async-done(((f32[8,2,256]{2,1,0:T(2,128)}), f32[8,2,256]{2,1,0:T(2,128)S(1)}, u32[]{:S(2)}, u32[]{:S(2)}) %all-to-all-start) | async-done | bytes 16416 | tf_op jit(solution)/shard_map/all_to_all | solution.py:134
  12.1 0.0 copy-start.3
  12.1 0.7 %copy-done.3 = s32[1,8,8]{2,1,0:T(8,128)S(1)} copy-done((s32[1,8,8]{2,1,0:T(8,128)S(1)}, s32[1,8,8]{2,1,0:T(8,128)}, u32[]{:S(2)}) %copy-start.3) | copy-done | bytes 280
  12.8 0.0 copy-start
  12.8 1.2 %copy-done = bf16[2,1,128,2048]{3,2,1,0:T(8,128)(2,1)S(1)} copy-done((bf16[2,1,128,2048]{3,2,1,0:T(8,128)(2,1)S(1)}, bf16[2,1,128,2048]{3,2,1,0:T(8,128)(2,1)}, u32[]{:S(2)}) %copy-start) | copy-done | bytes 1048600
  14.0 0.0 copy-start.1
  14.0 2.3 %shard_map.64 = (bf16[256,256]{1,0:T(8,128)(2,1)S(1)}, bf16[256,256]{1,0:T(8,128)(2,1)S(1)}, bf16[256,256]{1,0:T(8,128)(2,1)S(1)}, bf16[256,256]{1,0:T(8,128)(2,...) custom-call(s32[8,8]{1,0:T(8,128)S(1)} %bitcast.17, ...), custom_call_target="tpu_custom_call" | custom-call | tf_op jit(solution)/shard_map/pallas_call | solution.py:137
  16.3 0.1 collective-permute-start
  16.4 1.9 %collective-permute-start.1 = (bf16[256,256]{1,0:T(8,128)(2,1)S(1)}, bf16[256,256]{1,0:T(8,128)(2,1)S(1)}, u32[]{:S(2)}, u32[]{:S(2)}) collective-permute-start(bf16[256,256]{1,0:T(8,128)(2,1)S(1)} %get-tuple-element.19), channel_id=1, source_target_pairs={{0,2},{1,3},{2,0},{3,1},{4,6},{5,7},{6,4},{7,5},{8,10},{9,11},{10,... | collective-permute-start | bytes 393224 | tf_op jit(solution)/shard_map/ppermute | solution.py:146
  18.3 0.1 collective-permute-start.2
  18.4 1.3 %collective-permute-start.3 = (bf16[256,256]{1,0:T(8,128)(2,1)S(1)}, bf16[256,256]{1,0:T(8,128)(2,1)S(1)}, u32[]{:S(2)}, u32[]{:S(2)}) collective-permute-start(bf16[256,256]{1,0:T(8,128)(2,1)S(1)} %get-tuple-element.21), channel_id=1, source_target_pairs={{0,4},{1,5},{2,6},{3,7},{4,0},{5,1},{6,2},{7,3},{8,12},{9,13},{10,... | collective-permute-start | bytes 393224 | tf_op jit(solution)/shard_map/ppermute | solution.py:146
  19.7 0.3 collective-permute-start.4
  19.9 0.0 collective-permute-done.refs_1_
  19.9 1.7 %collective-permute-start.5 = (bf16[256,256]{1,0:T(8,128)(2,1)S(1)}, bf16[256,256]{1,0:T(8,128)(2,1)S(1)}, u32[]{:S(2)}, u32[]{:S(2)}) collective-permute-start(bf16[256,256]{1,0:T(8,128)(2,1)S(1)} %get-tuple-element.23), channel_id=1, source_target_pairs={{0,6},{1,7},{2,4},{3,5},{4,2},{5,3},{6,0},{7,1},{8,14},{9,15},{10,... | collective-permute-start | bytes 393224 | tf_op jit(solution)/shard_map/ppermute | solution.py:146
  21.6 1.1 %collective-permute-done.1.refs_2_ = bf16[256,256]{1,0:T(8,128)(2,1)S(1)} collective-permute-done((bf16[256,256]{1,0:T(8,128)(2,1)S(1)}, bf16[256,256]{1,0:T(8,128)(2,1)S(1)}, u32[]{:S(2)}, u32[]{:S(2)}) %collective-permute-start.1) | collective-permute-done | bytes 131104 | tf_op jit(solution)/shard_map/ppermute | solution.py:146
  22.7 0.2 collective-permute-start.6
  22.9 2.1 %collective-permute-done.2.refs_3_ = bf16[256,256]{1,0:T(8,128)(2,1)S(1)} collective-permute-done((bf16[256,256]{1,0:T(8,128)(2,1)S(1)}, bf16[256,256]{1,0:T(8,128)(2,1)S(1)}, u32[]{:S(2)}, u32[]{:S(2)}) %collective-permute-start.2) | collective-permute-done | bytes 131104 | tf_op jit(solution)/shard_map/ppermute | solution.py:146
  24.9 0.0 collective-permute-done.3.refs_4_
  24.9 6.4 %collective-permute-done.4.refs_5_ = bf16[256,256]{1,0:T(8,128)(2,1)S(1)} collective-permute-done((bf16[256,256]{1,0:T(8,128)(2,1)S(1)}, bf16[256,256]{1,0:T(8,128)(2,1)S(1)}, u32[]{:S(2)}, u32[]{:S(2)}) %collective-permute-start.4) | collective-permute-done | bytes 131104 | tf_op jit(solution)/shard_map/ppermute | solution.py:146
  31.4 0.0 collective-permute-done.5.refs_6_
  31.4 0.0 collective-permute-done.6.refs_7_
  31.4 0.0 copy-done.1
  31.4 0.8 %shard_map.65 = (f32[2,64,384]{2,1,0:T(8,128)S(1)}, bf16[2,64,384]{2,1,0:T(8,128)(2,1)S(1)}, bf16[2,64,384]{2,1,0:T(8,128)(2,1)S(1)}, bf16[2,64,384]{2,1,0:T(8,128)(2,1)S(1)}) custom-call(bf16[8,384,128]{2,1,0:T(8,128)(2,1)S(1)} %bitcast.16, bf16[256,256]{1,0:T(8,128)(2,1)S(1)} %get-tuple-element.17.refs_0_, ...), custom_call_target="tpu_custom_call" | custom-call | tf_op jit(solution)/shard_map/pallas_call | solution.py:150
  32.1 0.0 copy-start.2
  32.2 0.7 %copy-done.2 = f32[2,64,384]{2,1,0:T(8,128)} copy-done((f32[2,64,384]{2,1,0:T(8,128)}, f32[2,64,384]{2,1,0:T(8,128)S(1)}, u32[]{:S(2)}) %copy-start.2) | copy-done | bytes 196632
  32.8 2.9 %collective-permute-start.7 = (bf16[2,64,384]{2,1,0:T(8,128)(2,1)S(1)}, bf16[2,64,384]{2,1,0:T(8,128)(2,1)S(1)}, u32[]{:S(2)}, u32[]{:S(2)}) collective-permute-start(bf16[2,64,384]{2,1,0:T(8,128)(2,1)S(1)} %get-tuple-element.26), channel_id=1, source_target_pairs={{0,8},{8,0},{16,24},{24,16},{1,9},{9,1},{17,25},{25,17},{2,10},{10... | collective-permute-start | bytes 294920 | tf_op jit(solution)/shard_map/ppermute | solution.py:160
  35.8 2.2 %collective-permute-start.8 = (bf16[2,64,384]{2,1,0:T(8,128)(2,1)S(1)}, bf16[2,64,384]{2,1,0:T(8,128)(2,1)S(1)}, u32[]{:S(2)}, u32[]{:S(2)}) collective-permute-start(bf16[2,64,384]{2,1,0:T(8,128)(2,1)S(1)} %get-tuple-element.27), channel_id=1, source_target_pairs={{0,16},{8,24},{16,0},{24,8},{1,17},{9,25},{17,1},{25,9},{2,18},{10... | collective-permute-start | bytes 294920 | tf_op jit(solution)/shard_map/ppermute | solution.py:160
  37.9 0.2 collective-permute-start.9
  38.1 0.7 %collective-permute-done.7.refs_1_ = bf16[2,64,384]{2,1,0:T(8,128)(2,1)S(1)} collective-permute-done((bf16[2,64,384]{2,1,0:T(8,128)(2,1)S(1)}, bf16[2,64,384]{2,1,0:T(8,128)(2,1)S(1)}, u32[]{:S(2)}, u32[]{:S(2)}) %collective-permute-start.7) | collective-permute-done | bytes 98336 | tf_op jit(solution)/shard_map/ppermute | solution.py:160
  38.8 0.0 copy-start.4
  38.8 7.6 %collective-permute-done.8.refs_2_ = bf16[2,64,384]{2,1,0:T(8,128)(2,1)S(1)} collective-permute-done((bf16[2,64,384]{2,1,0:T(8,128)(2,1)S(1)}, bf16[2,64,384]{2,1,0:T(8,128)(2,1)S(1)}, u32[]{:S(2)}, u32[]{:S(2)}) %collective-permute-start.8) | collective-permute-done | bytes 98336 | tf_op jit(solution)/shard_map/ppermute | solution.py:160
  46.4 0.0 copy-start.5
  46.4 0.0 collective-permute-done.9.refs_3_
  46.4 0.0 copy-start.6
  46.4 0.0 copy-done.4
  46.4 0.6 %copy-done.5 = bf16[2,64,384]{2,1,0:T(8,128)(2,1)} copy-done((bf16[2,64,384]{2,1,0:T(8,128)(2,1)}, bf16[2,64,384]{2,1,0:T(8,128)(2,1)S(1)}, u32[]{:S(2)}) %copy-start.5) | copy-done | bytes 98328
  47.1 0.0 copy-done.6
  47.1 2.0 %shard_map.66 = f32[64,384]{1,0:T(8,128)} custom-call(f32[2,64,384]{2,1,0:T(8,128)} %copy-done.2, bf16[2,64,384]{2,1,0:T(8,128)(2,1)} %copy-done.4, bf16[2,64,384]{2,1,0:T(8,128)(2,1)} %copy-done.5, bf16[2,64,384]{2,1,0:T(8,128)(2,1)} %copy-done.6), custom_call_target="tpu_custom_call" | custom-call | tf_op jit(solution)/shard_map/pallas_call | solution.py:162
  (4 shorter events, 0.0 us)
Async XLA Ops:
  0.7 0.7 %copy-start.7 = (bf16[1,1,8,256]{3,2,1,0:T(8,128)(2,1)S(1)}, bf16[1,1,8,256]{3,2,1,0:T(8,128)(2,1)}, u32[]{:S(2)}) copy-start(bf16[1,1,8,256]{3,2,1,0:T(8,128)(2,1)} %param.9) | copy-start | bytes 12292
  2.0 5.3 %copy-start.8 = (s32[1,8,4]{1,2,0:T(4,128)S(1)}, s32[1,8,4]{1,2,0:T(4,128)}, u32[]{:S(2)}) copy-start(s32[1,8,4]{1,2,0:T(4,128)} %param.10) | copy-start | bytes 388
  2.0 10.1 %all-to-all-start = ((f32[8,2,256]{2,1,0:T(2,128)}), f32[8,2,256]{2,1,0:T(2,128)S(1)}, u32[]{:S(2)}, u32[]{:S(2)}) async-start(f32[8,2,256]{2,1,0:T(2,128)} %pad_maximum_fusion), calls=%async_computation | async-start | bytes 32768 | tf_op jit(solution)/shard_map/all_to_all | solution.py:134
  12.1 0.7 %copy-start.3 = (s32[1,8,8]{2,1,0:T(8,128)S(1)}, s32[1,8,8]{2,1,0:T(8,128)}, u32[]{:S(2)}) copy-start(s32[1,8,8]{2,1,0:T(8,128)} %param.7) | copy-start | bytes 772
  12.8 1.2 %copy-start = (bf16[2,1,128,2048]{3,2,1,0:T(8,128)(2,1)S(1)}, bf16[2,1,128,2048]{3,2,1,0:T(8,128)(2,1)}, u32[]{:S(2)}) copy-start(bf16[2,1,128,2048]{3,2,1,0:T(8,128)(2,1)} %param.6) | copy-start | bytes 3145732
  14.0 17.3 %copy-start.1 = (bf16[1,1,8,384,128]{4,3,2,1,0:T(8,128)(2,1)S(1)}, bf16[1,1,8,384,128]{4,3,2,1,0:T(8,128)(2,1)}, u32[]{:S(2)}) copy-start(bf16[1,1,8,384,128]{4,3,2,1,0:T(8,128)(2,1)} %param.11) | copy-start | bytes 2359300
  16.3 3.6 %collective-permute-start = (bf16[256,256]{1,0:T(8,128)(2,1)S(1)}, bf16[256,256]{1,0:T(8,128)(2,1)S(1)}, u32[]{:S(2)}, u32[]{:S(2)}) collective-permute-start(bf16[256,256]{1,0:T(8,128)(2,1)S(1)} %get-tuple-element.18), channel_id=1, source_target_pairs={{0,1},{1,0},{2,3},{3,2},{4,5},{5,4},{6,7},{7,6},{8,9},{9,8},{10,11... | collective-permute-start | bytes 393224 | tf_op jit(solution)/shard_map/ppermute | solution.py:146
  16.4 6.3 %collective-permute-start.1 = (bf16[256,256]{1,0:T(8,128)(2,1)S(1)}, bf16[256,256]{1,0:T(8,128)(2,1)S(1)}, u32[]{:S(2)}, u32[]{:S(2)}) collective-permute-start(bf16[256,256]{1,0:T(8,128)(2,1)S(1)} %get-tuple-element.19), channel_id=1, source_target_pairs={{0,2},{1,3},{2,0},{3,1},{4,6},{5,7},{6,4},{7,5},{8,10},{9,11},{10,... | collective-permute-start | bytes 393224 | tf_op jit(solution)/shard_map/ppermute | solution.py:146
  18.3 6.6 %collective-permute-start.2 = (bf16[256,256]{1,0:T(8,128)(2,1)S(1)}, bf16[256,256]{1,0:T(8,128)(2,1)S(1)}, u32[]{:S(2)}, u32[]{:S(2)}) collective-permute-start(bf16[256,256]{1,0:T(8,128)(2,1)S(1)} %get-tuple-element.20), channel_id=1, source_target_pairs={{0,3},{1,2},{2,1},{3,0},{4,7},{5,6},{6,5},{7,4},{8,11},{9,10},{10,... | collective-permute-start | bytes 393224 | tf_op jit(solution)/shard_map/ppermute | solution.py:146
  18.4 6.6 %collective-permute-start.3 = (bf16[256,256]{1,0:T(8,128)(2,1)S(1)}, bf16[256,256]{1,0:T(8,128)(2,1)S(1)}, u32[]{:S(2)}, u32[]{:S(2)}) collective-permute-start(bf16[256,256]{1,0:T(8,128)(2,1)S(1)} %get-tuple-element.21), channel_id=1, source_target_pairs={{0,4},{1,5},{2,6},{3,7},{4,0},{5,1},{6,2},{7,3},{8,12},{9,13},{10,... | collective-permute-start | bytes 393224 | tf_op jit(solution)/shard_map/ppermute | solution.py:146
  19.7 11.7 %collective-permute-start.4 = (bf16[256,256]{1,0:T(8,128)(2,1)S(1)}, bf16[256,256]{1,0:T(8,128)(2,1)S(1)}, u32[]{:S(2)}, u32[]{:S(2)}) collective-permute-start(bf16[256,256]{1,0:T(8,128)(2,1)S(1)} %get-tuple-element.22), channel_id=1, source_target_pairs={{0,5},{1,4},{2,7},{3,6},{4,1},{5,0},{6,3},{7,2},{8,13},{9,12},{10,... | collective-permute-start | bytes 393224 | tf_op jit(solution)/shard_map/ppermute | solution.py:146
  19.9 11.4 %collective-permute-start.5 = (bf16[256,256]{1,0:T(8,128)(2,1)S(1)}, bf16[256,256]{1,0:T(8,128)(2,1)S(1)}, u32[]{:S(2)}, u32[]{:S(2)}) collective-permute-start(bf16[256,256]{1,0:T(8,128)(2,1)S(1)} %get-tuple-element.23), channel_id=1, source_target_pairs={{0,6},{1,7},{2,4},{3,5},{4,2},{5,3},{6,0},{7,1},{8,14},{9,15},{10,... | collective-permute-start | bytes 393224 | tf_op jit(solution)/shard_map/ppermute | solution.py:146
  22.7 8.6 %collective-permute-start.6 = (bf16[256,256]{1,0:T(8,128)(2,1)S(1)}, bf16[256,256]{1,0:T(8,128)(2,1)S(1)}, u32[]{:S(2)}, u32[]{:S(2)}) collective-permute-start(bf16[256,256]{1,0:T(8,128)(2,1)S(1)} %get-tuple-element.24), channel_id=1, source_target_pairs={{0,7},{1,6},{2,5},{3,4},{4,3},{5,2},{6,1},{7,0},{8,15},{9,14},{10,... | collective-permute-start | bytes 393224 | tf_op jit(solution)/shard_map/ppermute | solution.py:146
  32.1 0.7 %copy-start.2 = (f32[2,64,384]{2,1,0:T(8,128)}, f32[2,64,384]{2,1,0:T(8,128)S(1)}, u32[]{:S(2)}) copy-start(f32[2,64,384]{2,1,0:T(8,128)S(1)} %get-tuple-element.25.refs_0_) | copy-start | bytes 589828
  32.8 6.0 %collective-permute-start.7 = (bf16[2,64,384]{2,1,0:T(8,128)(2,1)S(1)}, bf16[2,64,384]{2,1,0:T(8,128)(2,1)S(1)}, u32[]{:S(2)}, u32[]{:S(2)}) collective-permute-start(bf16[2,64,384]{2,1,0:T(8,128)(2,1)S(1)} %get-tuple-element.26), channel_id=1, source_target_pairs={{0,8},{8,0},{16,24},{24,16},{1,9},{9,1},{17,25},{25,17},{2,10},{10... | collective-permute-start | bytes 294920 | tf_op jit(solution)/shard_map/ppermute | solution.py:160
  35.8 10.7 %collective-permute-start.8 = (bf16[2,64,384]{2,1,0:T(8,128)(2,1)S(1)}, bf16[2,64,384]{2,1,0:T(8,128)(2,1)S(1)}, u32[]{:S(2)}, u32[]{:S(2)}) collective-permute-start(bf16[2,64,384]{2,1,0:T(8,128)(2,1)S(1)} %get-tuple-element.27), channel_id=1, source_target_pairs={{0,16},{8,24},{16,0},{24,8},{1,17},{9,25},{17,1},{25,9},{2,18},{10... | collective-permute-start | bytes 294920 | tf_op jit(solution)/shard_map/ppermute | solution.py:160
  37.9 8.5 %collective-permute-start.9 = (bf16[2,64,384]{2,1,0:T(8,128)(2,1)S(1)}, bf16[2,64,384]{2,1,0:T(8,128)(2,1)S(1)}, u32[]{:S(2)}, u32[]{:S(2)}) collective-permute-start(bf16[2,64,384]{2,1,0:T(8,128)(2,1)S(1)} %get-tuple-element.28), channel_id=1, source_target_pairs={{0,24},{8,16},{16,8},{24,0},{1,25},{9,17},{17,9},{25,1},{2,26},{10... | collective-permute-start | bytes 294920 | tf_op jit(solution)/shard_map/ppermute | solution.py:160
  38.8 7.6 %copy-start.4 = (bf16[2,64,384]{2,1,0:T(8,128)(2,1)}, bf16[2,64,384]{2,1,0:T(8,128)(2,1)S(1)}, u32[]{:S(2)}) copy-start(bf16[2,64,384]{2,1,0:T(8,128)(2,1)S(1)} %collective-permute-done.7.refs_1_) | copy-start | bytes 294916
  46.4 0.6 %copy-start.5 = (bf16[2,64,384]{2,1,0:T(8,128)(2,1)}, bf16[2,64,384]{2,1,0:T(8,128)(2,1)S(1)}, u32[]{:S(2)}) copy-start(bf16[2,64,384]{2,1,0:T(8,128)(2,1)S(1)} %collective-permute-done.8.refs_2_) | copy-start | bytes 294916
  46.4 0.7 %copy-start.6 = (bf16[2,64,384]{2,1,0:T(8,128)(2,1)}, bf16[2,64,384]{2,1,0:T(8,128)(2,1)S(1)}, u32[]{:S(2)}) copy-start(bf16[2,64,384]{2,1,0:T(8,128)(2,1)S(1)} %collective-permute-done.9.refs_3_) | copy-start | bytes 294916

commit v2 on v0

v2 whole, which is shorter than its diff:
```python
import functools

import jax
import jax.numpy as jnp
from jax import lax
from jax.experimental import pallas as pl
from jax.experimental.pallas import tpu as pltpu
from jax.sharding import PartitionSpec as P

TW = 512
LANES = 128
SLAB = TW + LANES
CHUNKS = 1
NT_DIMS = (((1,), (1,)), ((), ()))
VMEM = pl.BlockSpec(memory_space=pltpu.VMEM)
SMEM = pl.BlockSpec(memory_space=pltpu.SMEM)


def target_of(pos, step, count):
    if count & (count - 1) == 0:
        return pos ^ step
    return (pos + step) % count


def source_of(pos, step, count):
    if count & (count - 1) == 0:
        return pos ^ step
    return (pos - step + count) % count


def pairs(step, count):
    return [(pos, target_of(pos, step, count)) for pos in range(count)]


def chip_pairs(step, tiles):
    return [
        (pos, 2 * target_of(pos // 2, step, tiles // 2) + pos % 2) for pos in range(tiles)
    ]


def steps_of(count):
    return list(range(count - 1, 0, -1))


def wanted_kernel(tiles, index_ref, frac_ref, *out_refs):
    me = lax.axis_index("tile")
    rows = index_ref[...].astype(jnp.float32)
    weights = frac_ref[...].astype(jnp.float32)
    position = lax.broadcasted_iota(jnp.int32, rows.shape, 0)
    for step, out_ref in enumerate(out_refs):
        block = 2 * source_of(me // 2, step, tiles // 2) + me % 2 if step else me
        for other in range(2):
            mine = position == (block ^ other)
            out_ref[other : other + 1] = jnp.sum(
                jnp.where(mine, rows, 0.0), axis=0, keepdims=True
            )
            out_ref[2 + other : 3 + other] = jnp.sum(
                jnp.where(mine, weights, 0.0), axis=0, keepdims=True
            )


def depth_kernel(tiles, shots, chunks, steps, start_ref, aperture_ref, own_ref, other_ref, *refs):
    me = lax.axis_index("tile")
    wanted_refs, out_refs = refs[: len(steps)], refs[len(steps) :]
    samples = own_ref.shape[2]
    depth = wanted_refs[0].shape[1]
    piece = depth // shots
    span = piece // chunks
    lane = lax.broadcasted_iota(jnp.int32, (depth // chunks, SLAB), 1).astype(jnp.float32)
    for place, step in enumerate(steps):
        tile = 2 * target_of(me // 2, step, tiles // 2) + me % 2 if step else me
        columns = wanted_refs[place][...].T
        for other, traces_ref in enumerate((own_ref, other_ref)):
            block = me ^ other
            listed = aperture_ref[tile, 0] == block
            for slot in range(1, aperture_ref.shape[1]):
                listed = jnp.logical_or(listed, aperture_ref[tile, slot] == block)
            outs = out_refs[place * chunks : (place + 1) * chunks]

            @pl.when(listed)
            def _():
                first = start_ref[tile, block]
                slab = jnp.minimum(first // LANES, (samples - SLAB) // LANES) * LANES
                slab = pl.multiple_of(slab, LANES)
                window = jnp.concatenate(
                    [traces_ref[0, :, pl.ds(slab, SLAB)], traces_ref[1, :, pl.ds(slab, SLAB)]],
                    axis=0,
                )
                shift = (first - slab).astype(jnp.float32)
                for chunk in range(chunks):
                    mine = jnp.concatenate(
                        [
                            columns[shot * piece + chunk * span : shot * piece + (chunk + 1) * span]
                            for shot in range(shots)
                        ],
                        axis=0,
                    )
                    row = mine[:, other : other + 1] + shift
                    weight = mine[:, 2 + other : 3 + other]
                    lower_hot = (lane == row).astype(jnp.bfloat16)
                    upper_hot = (lane == row + 1.0).astype(jnp.bfloat16)
                    lower = lax.dot_general(
                        lower_hot, window, NT_DIMS, preferred_element_type=jnp.float32
                    )
                    upper = lax.dot_general(
                        upper_hot, window, NT_DIMS, preferred_element_type=jnp.float32
                    )
                    outs[chunk][other] = ((1.0 - weight) * lower + weight * upper).astype(
                        jnp.bfloat16
                    )

            @pl.when(jnp.logical_not(listed))
            def _():
                for out_ref in outs:
                    out_ref[other] = jnp.zeros(out_ref.shape[1:], out_ref.dtype)


def partial_kernel(tiles, shots, steps, amplitude_ref, *refs):
    me = lax.axis_index("tile")
    my_shot = lax.axis_index("shot")
    depth_refs = refs[: len(steps)]
    own_ref, out_refs, total_ref = refs[len(steps)], refs[len(steps) + 1 : -1], refs[-1]
    receivers = amplitude_ref.shape[2]
    span = own_ref.shape[1]
    group = 4
    for base in range(0, len(steps), group):
        places = range(base, min(base + group, len(steps)))
        weights = []
        for place in places:
            step = steps[place]
            block = 2 * source_of(me // 2, step, tiles // 2) + me % 2 if step else me
            weights += [amplitude_ref[block], amplitude_ref[block ^ 1]]
        weights = jnp.concatenate(weights, axis=1)
        for part in range(2):
            lanes = slice(part * receivers, (part + 1) * receivers)
            traces = jnp.concatenate(
                [depth_refs[place][other, :, lanes] for place in places for other in range(2)],
                axis=1,
            )
            added = lax.dot_general(traces, weights, NT_DIMS, preferred_element_type=jnp.float32)
            if base:
                added = added + total_ref[part]
            total_ref[part] = added
    for part in range(2):
        own_ref[part] = total_ref[part, pl.ds(pl.multiple_of(my_shot * span, span), span), :]
        for place, step in enumerate(steps_of(shots)):
            target = target_of(my_shot, step, shots)
            rows = pl.ds(pl.multiple_of(target * span, span), span)
            out_refs[place][part] = total_ref[part, rows, :].astype(jnp.bfloat16)


def image_kernel(shots, chunks, *refs):
    out_ref = refs[-1]
    for chunk in range(chunks):
        stack = None
        for ref in refs[chunk * shots : (chunk + 1) * shots]:
            real = ref[0].astype(jnp.float32)
            imag = ref[1].astype(jnp.float32)
            inverse = 1.0 / jnp.maximum(jnp.sqrt(real * real + imag * imag), 1.0)
            if stack is None:
                stack, first, second = real, real * inverse, imag * inverse
            else:
                stack = stack + real
                first = first + real * inverse
                second = second + imag * inverse
        span = stack.shape[0]
        out_ref[chunk * span : (chunk + 1) * span] = (
            stack * (first * first + second * second) / (shots * shots)
        )


def local(traces, start, depth_index, depth_frac, aperture, amplitude):
    tiles = lax.axis_size("tile")
    shots = lax.axis_size("shot")
    parts, _, receivers, samples = traces.shape
    depth = depth_index.shape[3]
    columns = amplitude.shape[3]
    piece = depth // shots
    chunks = CHUNKS if piece % (16 * CHUNKS) == 0 else 1
    span = piece // chunks
    away = steps_of(tiles // 2)
    params = pltpu.CompilerParams(vmem_limit_bytes=32 << 20)
    small = pltpu.CompilerParams(vmem_limit_bytes=8 << 20)

    own_traces = traces[:, 0]
    other_traces = lax.ppermute(own_traces, "tile", [(pos, pos ^ 1) for pos in range(tiles)])

    wanted = pl.pallas_call(
        functools.partial(wanted_kernel, tiles),
        out_shape=[jax.ShapeDtypeStruct((4, depth), jnp.float32)] * (tiles // 2),
        in_specs=[VMEM, VMEM],
        out_specs=[VMEM] * (tiles // 2),
        compiler_params=small,
    )(depth_index[0, 0], depth_frac[0, 0])
    asked = [lax.ppermute(wanted[step], "tile", chip_pairs(step, tiles)) for step in away]

    def depth_traces(steps, requests):
        block = jax.ShapeDtypeStruct((2, depth // chunks, parts * receivers), jnp.bfloat16)
        return pl.pallas_call(
            functools.partial(depth_kernel, tiles, shots, chunks, steps),
            out_shape=[block] * (len(steps) * chunks),
            in_specs=[SMEM, SMEM, VMEM, VMEM] + [VMEM] * len(steps),
            out_specs=[VMEM] * (len(steps) * chunks),
            compiler_params=params,
        )(start[0], aperture[0], own_traces, other_traces, *requests)

    kept = depth_traces([0], [wanted[0]])
    sent = depth_traces(away, asked)

    own = jax.ShapeDtypeStruct((parts, span, columns), jnp.float32)
    other = jax.ShapeDtypeStruct((parts, span, columns), jnp.bfloat16)
    received = [
        [
            lax.ppermute(sent[place * chunks + chunk], "tile", chip_pairs(step, tiles))
            for place, step in enumerate(away)
        ]
        for chunk in range(chunks)
    ]
    summed = []
    for chunk in range(chunks):
        pieces = pl.pallas_call(
            functools.partial(partial_kernel, tiles, shots, [0] + away),
            out_shape=[own] + [other] * (shots - 1),
            in_specs=[VMEM] * (1 + tiles // 2),
            out_specs=[VMEM] * shots,
            scratch_shapes=[pltpu.VMEM((parts, depth // chunks, columns), jnp.float32)],
            compiler_params=params,
        )(amplitude[0, 0], kept[chunk], *received[chunk])
        summed.append(pieces[0])
        for place, step in enumerate(steps_of(shots)):
            summed.append(lax.ppermute(pieces[1 + place], "shot", pairs(step, shots)))

    image = pl.pallas_call(
        functools.partial(image_kernel, shots, chunks),
        out_shape=jax.ShapeDtypeStruct((piece, columns), jnp.float32),
        in_specs=[VMEM] * (shots * chunks),
        out_specs=VMEM,
        compiler_params=small,
    )(*summed)
    return image.T


def solution(mesh):
    in_specs = (
        P(None, "shot", "tile", None),
        P("shot", None, None),
        P("shot", "tile", None, None),
        P("shot", "tile", None, None),
        P("shot", None, None),
        P("shot", "tile", None, None, None),
    )
    out_specs = P("tile", "shot")
    return jax.shard_map(local, mesh=mesh, in_specs=in_specs, out_specs=out_specs, check_vma=False)
```

time: 146 us -> 40 us (0.27)
  waiting for transfers between devices: 85.7 us -> 18.4 us
  loops' own time: 14.8 us -> 0 us
  local copies, waits for them, and re-layouts: 15.7 us -> 2.27 us
  between operations: 13.2 us -> 0.05 us
  starting transfers between devices: 5.42 us -> 15.1 us
  other arithmetic: 6.88 us -> 0 us
  Pallas kernels: 0 us -> 3.66 us
  matrix products: 3.61 us -> 0 us
    reduce_scatter x3 -> x0, waiting for transfers between devices: 61 us -> none  [the longest x1 21.2 us: local(): lax.psum_scatter(partial_value[1] * inverse, 'shot', scatter_dimension=1,...]
    all_to_all x1 -> x0, waiting for transfers between devices: 24 us -> none  [local(): lax.all_to_all(windows, 'tile', split_axis=0, concat_axis=0, tiled=True)]
    ppermute x0 -> x10, waiting for transfers between devices: none -> 18.4 us  [the longest x3 8.29 us: local(): lax.ppermute(sent[place * chunks + chunk], 'tile', chip_pairs(step, tiles))]
    ppermute x0 -> x10, starting transfers between devices: none -> 15.1 us  [the longest x3 5.58 us: local(): lax.ppermute(sent[place * chunks + chunk], 'tile', chip_pairs(step, tiles))]
    another operation x1 -> x0, loops' own time: 14.8 us -> none  [local(): windows = lax.fori_loop(0, tile_count, cut_window, empty)]
    dynamic_update_slice x8 -> x0, local copies, waits for them, and re-layouts: 8.98 us -> none  [cut_window(): return lax.dynamic_update_index_in_dim(filled, piece, block_pos, 0)]
    dynamic_slice x9 -> x0, local copies, waits for them, and re-layouts: 5.89 us -> none  [the longest x8 4.93 us: cut_window(): first_sample = my_starts[block_pos]]
    all_to_all x1 -> x0, starting transfers between devices: 5.3 us -> none  [local(): lax.all_to_all(windows, 'tile', split_axis=0, concat_axis=0, tiled=True)]
  transfers between devices with their start and end apart: 4 -> 10, of which waited for: 4 -> 8; matrix products, arithmetic and copies ran while one was open for 2% -> 0% of each run, Pallas kernels for 0% -> 2%
where the time goes in v2:
time: 40 us; the launch traced here: 39.4 us
  waiting for transfers between devices  18.4 us (46%)
  starting transfers between devices  15.1 us (38%)
  Pallas kernels  3.66 us (9%)
  local copies, waits for them, and re-layouts  2.27 us (6%)
    ppermute x3, waiting for transfers between devices, local(): lax.ppermute(sent[place * chunks + chunk], 'tile', chip_pairs(step, tiles))  8.29 us
    ppermute x3, waiting for transfers between devices, local(): summed.append(lax.ppermute(pieces[1 + place], 'shot', pairs(step, shots)))  6.73 us
    ppermute x3, starting transfers between devices, local(): lax.ppermute(sent[place * chunks + chunk], 'tile', chip_pairs(step, tiles))  5.58 us
    ppermute x3, starting transfers between devices, local(): lax.ppermute(wanted[step], 'tile', chip_pairs(step, tiles))  4.61 us
    ppermute x3, starting transfers between devices, local(): summed.append(lax.ppermute(pieces[1 + place], 'shot', pairs(step, shots)))  4.45 us
    ppermute x3, waiting for transfers between devices, local(): lax.ppermute(wanted[step], 'tile', chip_pairs(step, tiles))  3.35 us
    unnamed x14, local copies, waits for them, and re-layouts  2.19 us
    pallas_call x2, Pallas kernels, depth_traces(): pl.pallas_call(functools.partial(depth_kernel, tiles, shots, chunks, step...  1.95 us
  transfers between devices with their start and end apart: 10, of which 8 were waited for; matrix products, arithmetic and copies ran while one was open for 0% of the time, Pallas kernels for 2%

profile of v2, /device:TPU:0, one launch (start us, length us, event | category | flops | bytes accessed | tf_op | source)
XLA Modules:
  0.0 39.4 jit_solution(15844563441240126905)
XLA Ops:
  0.0 0.0 copy-start.5
  0.0 0.5 %collective-permute-start = (bf16[2,128,2048]{2,1,0:T(8,128)(2,1)}, bf16[2,128,2048]{2,1,0:T(8,128)(2,1)S(1)}, u32[]{:S(2)}, u32[]{:S(2)}) collective-permute-start(bf16[2,128,2048]{2,1,0:T(8,128)(2,1)} %bitcast.7), channel_id=1, source_target_pairs={{0,1},{1,0},{2,3},{3,2},{4,5},{5,4},{6,7},{7,6},{8,9},{9,8},{10,11... | collective-permute-start | bytes 3145736 | tf_op jit(solution)/shard_map/ppermute | solution.py:186
  0.5 0.2 copy-done.5
  0.7 0.0 copy-start.4
  0.7 0.7 %copy-done.4 = s32[1,1,8,256]{3,2,1,0:T(8,128)S(1)} copy-done((s32[1,1,8,256]{3,2,1,0:T(8,128)S(1)}, s32[1,1,8,256]{3,2,1,0:T(8,128)}, u32[]{:S(2)}) %copy-start.4) | copy-done | bytes 8216
  1.4 4.0 %collective-permute-start.1 = (f32[4,256]{1,0:T(4,128)S(1)}, f32[4,256]{1,0:T(4,128)S(1)}, u32[]{:S(2)}, u32[]{:S(2)}) collective-permute-start(f32[4,256]{1,0:T(4,128)S(1)} %get-tuple-element.17), channel_id=1, source_target_pairs={{0,6},{1,7},{2,4},{3,5},{4,2},{5,3},{6,0},{7,1},{8,14},{9,15},{10,... | collective-permute-start | bytes 12296 | tf_op jit(solution)/shard_map/ppermute | solution.py:195
  5.4 0.0 copy-start.6
  5.4 0.5 %collective-permute-start.2 = (f32[4,256]{1,0:T(4,128)S(1)}, f32[4,256]{1,0:T(4,128)S(1)}, u32[]{:S(2)}, u32[]{:S(2)}) collective-permute-start(f32[4,256]{1,0:T(4,128)S(1)} %get-tuple-element.18), channel_id=1, source_target_pairs={{0,4},{1,5},{2,6},{3,7},{4,0},{5,1},{6,2},{7,3},{8,12},{9,13},{10,... | collective-permute-start | bytes 12296 | tf_op jit(solution)/shard_map/ppermute | solution.py:195
  5.9 0.1 collective-permute-start.3
  6.1 0.0 copy-done.6
  6.1 0.0 copy-start.3
  6.1 0.1 copy.7.aperture_ref
  6.2 0.8 %collective-permute-done.1.refs_0_ = f32[4,256]{1,0:T(4,128)S(1)} collective-permute-done((f32[4,256]{1,0:T(4,128)S(1)}, f32[4,256]{1,0:T(4,128)S(1)}, u32[]{:S(2)}, u32[]{:S(2)}) %collective-permute-start.1) | collective-permute-done | bytes 4128 | tf_op jit(solution)/shard_map/ppermute | solution.py:195
  7.0 2.0 %collective-permute-done.2.refs_1_ = f32[4,256]{1,0:T(4,128)S(1)} collective-permute-done((f32[4,256]{1,0:T(4,128)S(1)}, f32[4,256]{1,0:T(4,128)S(1)}, u32[]{:S(2)}, u32[]{:S(2)}) %collective-permute-start.2) | collective-permute-done | bytes 4128 | tf_op jit(solution)/shard_map/ppermute | solution.py:195
  9.0 0.5 %collective-permute-done.3.refs_2_ = f32[4,256]{1,0:T(4,128)S(1)} collective-permute-done((f32[4,256]{1,0:T(4,128)S(1)}, f32[4,256]{1,0:T(4,128)S(1)}, u32[]{:S(2)}, u32[]{:S(2)}) %collective-permute-start.3) | collective-permute-done | bytes 4128 | tf_op jit(solution)/shard_map/ppermute | solution.py:195
  9.5 0.0 collective-permute-done.other_ref
  9.5 0.0 copy-done.3
  9.5 0.0 copy-start
  9.5 1.2 %copy-done = bf16[2,1,128,2048]{3,2,1,0:T(8,128)(2,1)S(1)} copy-done((bf16[2,1,128,2048]{3,2,1,0:T(8,128)(2,1)S(1)}, bf16[2,1,128,2048]{3,2,1,0:T(8,128)(2,1)}, u32[]{:S(2)}) %copy-start) | copy-done | bytes 1048600
  10.7 0.0 copy-start.1
  10.7 1.1 %shard_map.66 = (bf16[2,256,256]{2,1,0:T(8,128)(2,1)S(1)}, bf16[2,256,256]{2,1,0:T(8,128)(2,1)S(1)}, bf16[2,256,256]{2,1,0:T(8,128)(2,1)S(1)}) custom-call(s32[8,8]{1,0:T(8,128)S(1)} %bitcast.11, s32[8,4]{1,0:T(8,128)S(1)} %copy.7.aperture_ref, bf16[2,128,2048]{2,1,0:T(8,128)(2,1)S(1)} %bitcast.8, bf16[2,128,2048]{2,1,0:T(8,128)(2,1)S(1)} %collective-permute-done.other_ref, ...), custom_call_target="tpu_custom_call" | custom-call | tf_op jit(solution)/shard_map/pallas_call | solution.py:199
  11.9 2.8 %collective-permute-start.4 = (bf16[2,256,256]{2,1,0:T(8,128)(2,1)S(1)}, bf16[2,256,256]{2,1,0:T(8,128)(2,1)S(1)}, u32[]{:S(2)}, u32[]{:S(2)}) collective-permute-start(bf16[2,256,256]{2,1,0:T(8,128)(2,1)S(1)} %get-tuple-element.20), channel_id=1, source_target_pairs={{0,6},{1,7},{2,4},{3,5},{4,2},{5,3},{6,0},{7,1},{8,14},{9,15},{10,... | collective-permute-start | bytes 786440 | tf_op jit(solution)/shard_map/ppermute | solution.py:214
  14.7 1.4 %collective-permute-start.5 = (bf16[2,256,256]{2,1,0:T(8,128)(2,1)S(1)}, bf16[2,256,256]{2,1,0:T(8,128)(2,1)S(1)}, u32[]{:S(2)}, u32[]{:S(2)}) collective-permute-start(bf16[2,256,256]{2,1,0:T(8,128)(2,1)S(1)} %get-tuple-element.21), channel_id=1, source_target_pairs={{0,4},{1,5},{2,6},{3,7},{4,0},{5,1},{6,2},{7,3},{8,12},{9,13},{10,... | collective-permute-start | bytes 786440 | tf_op jit(solution)/shard_map/ppermute | solution.py:214
  16.1 1.4 %collective-permute-start.6 = (bf16[2,256,256]{2,1,0:T(8,128)(2,1)S(1)}, bf16[2,256,256]{2,1,0:T(8,128)(2,1)S(1)}, u32[]{:S(2)}, u32[]{:S(2)}) collective-permute-start(bf16[2,256,256]{2,1,0:T(8,128)(2,1)S(1)} %get-tuple-element.22), channel_id=1, source_target_pairs={{0,2},{1,3},{2,0},{3,1},{4,6},{5,7},{6,4},{7,5},{8,10},{9,11},{10,... | collective-permute-start | bytes 786440 | tf_op jit(solution)/shard_map/ppermute | solution.py:214
  17.5 0.0 copy-done.1
  17.5 0.0 copy-start.2
  17.5 0.8 %shard_map.65.refs_0_ = bf16[2,256,256]{2,1,0:T(8,128)(2,1)S(1)} custom-call(s32[8,8]{1,0:T(8,128)S(1)} %bitcast.12, s32[8,4]{1,0:T(8,128)S(1)} %copy.7.aperture_ref, bf16[2,128,2048]{2,1,0:T(8,128)(2,1)S(1)} %bitcast.9, bf16[2,128,2048]{2,1,0:T(8,128)(2,1)S(1)} %collective-permute-done.other_ref, f32[4,256]{1,0:T(4,128)S(1)} %get-tuple-element.16.refs_0_), custom_call_target="tpu_custom_call" | custom-call | tf_op jit(solution)/shard_map/pallas_call | solution.py:199
  18.3 3.8 %collective-permute-done.4.refs_1_ = bf16[2,256,256]{2,1,0:T(8,128)(2,1)S(1)} collective-permute-done((bf16[2,256,256]{2,1,0:T(8,128)(2,1)S(1)}, bf16[2,256,256]{2,1,0:T(8,128)(2,1)S(1)}, u32[]{:S(2)}, u32[]{:S(2)}) %collective-permute-start.4) | collective-permute-done | bytes 262176 | tf_op jit(solution)/shard_map/ppermute | solution.py:214
  22.1 3.4 %collective-permute-done.5.refs_2_ = bf16[2,256,256]{2,1,0:T(8,128)(2,1)S(1)} collective-permute-done((bf16[2,256,256]{2,1,0:T(8,128)(2,1)S(1)}, bf16[2,256,256]{2,1,0:T(8,128)(2,1)S(1)}, u32[]{:S(2)}, u32[]{:S(2)}) %collective-permute-start.5) | collective-permute-done | bytes 262176 | tf_op jit(solution)/shard_map/ppermute | solution.py:214
  25.5 1.1 %collective-permute-done.6.refs_3_ = bf16[2,256,256]{2,1,0:T(8,128)(2,1)S(1)} collective-permute-done((bf16[2,256,256]{2,1,0:T(8,128)(2,1)S(1)}, bf16[2,256,256]{2,1,0:T(8,128)(2,1)S(1)}, u32[]{:S(2)}, u32[]{:S(2)}) %collective-permute-start.6) | collective-permute-done | bytes 262176 | tf_op jit(solution)/shard_map/ppermute | solution.py:214
  26.6 0.0 copy-done.2
  26.6 0.8 %shard_map.67 = (f32[2,64,384]{2,1,0:T(8,128)S(1)}, bf16[2,64,384]{2,1,0:T(8,128)(2,1)S(1)}, bf16[2,64,384]{2,1,0:T(8,128)(2,1)S(1)}, bf16[2,64,384]{2,1,0:T(8,128)(2,1)S(1)}) custom-call(bf16[8,384,128]{2,1,0:T(8,128)(2,1)S(1)} %bitcast.10, bf16[2,256,256]{2,1,0:T(8,128)(2,1)S(1)} %shard_map.65.refs_0_, ...), custom_call_target="tpu_custom_call" | custom-call | tf_op jit(solution)/shard_map/pallas_call | solution.py:221
  27.4 2.9 %collective-permute-start.7 = (bf16[2,64,384]{2,1,0:T(8,128)(2,1)S(1)}, bf16[2,64,384]{2,1,0:T(8,128)(2,1)S(1)}, u32[]{:S(2)}, u32[]{:S(2)}) collective-permute-start(bf16[2,64,384]{2,1,0:T(8,128)(2,1)S(1)} %get-tuple-element.24), channel_id=1, source_target_pairs={{0,24},{8,16},{16,8},{24,0},{1,25},{9,17},{17,9},{25,1},{2,26},{10... | collective-permute-start | bytes 294920 | tf_op jit(solution)/shard_map/ppermute | solution.py:231
  30.2 1.1 %collective-permute-start.8 = (bf16[2,64,384]{2,1,0:T(8,128)(2,1)S(1)}, bf16[2,64,384]{2,1,0:T(8,128)(2,1)S(1)}, u32[]{:S(2)}, u32[]{:S(2)}) collective-permute-start(bf16[2,64,384]{2,1,0:T(8,128)(2,1)S(1)} %get-tuple-element.25), channel_id=1, source_target_pairs={{0,16},{8,24},{16,0},{24,8},{1,17},{9,25},{17,1},{25,9},{2,18},{10... | collective-permute-start | bytes 294920 | tf_op jit(solution)/shard_map/ppermute | solution.py:231
  31.3 0.5 %collective-permute-start.9 = (bf16[2,64,384]{2,1,0:T(8,128)(2,1)S(1)}, bf16[2,64,384]{2,1,0:T(8,128)(2,1)S(1)}, u32[]{:S(2)}, u32[]{:S(2)}) collective-permute-start(bf16[2,64,384]{2,1,0:T(8,128)(2,1)S(1)} %get-tuple-element.26), channel_id=1, source_target_pairs={{0,8},{8,0},{16,24},{24,16},{1,9},{9,1},{17,25},{25,17},{2,10},{10... | collective-permute-start | bytes 294920 | tf_op jit(solution)/shard_map/ppermute | solution.py:231
  31.8 3.1 %collective-permute-done.7.refs_1_ = bf16[2,64,384]{2,1,0:T(8,128)(2,1)S(1)} collective-permute-done((bf16[2,64,384]{2,1,0:T(8,128)(2,1)S(1)}, bf16[2,64,384]{2,1,0:T(8,128)(2,1)S(1)}, u32[]{:S(2)}, u32[]{:S(2)}) %collective-permute-start.7) | collective-permute-done | bytes 98336 | tf_op jit(solution)/shard_map/ppermute | solution.py:231
  34.9 3.7 %collective-permute-done.8.refs_2_ = bf16[2,64,384]{2,1,0:T(8,128)(2,1)S(1)} collective-permute-done((bf16[2,64,384]{2,1,0:T(8,128)(2,1)S(1)}, bf16[2,64,384]{2,1,0:T(8,128)(2,1)S(1)}, u32[]{:S(2)}, u32[]{:S(2)}) %collective-permute-start.8) | collective-permute-done | bytes 98336 | tf_op jit(solution)/shard_map/ppermute | solution.py:231
  38.5 0.0 collective-permute-done.9.refs_3_
  38.6 0.9 %shard_map.68 = f32[64,384]{1,0:T(8,128)} custom-call(f32[2,64,384]{2,1,0:T(8,128)S(1)} %get-tuple-element.23.refs_0_, bf16[2,64,384]{2,1,0:T(8,128)(2,1)S(1)} %collective-permute-done.7.refs_1_, bf16[2,64,384]{2,1,0:T(8,128)(2,1)S(1)} %collective-permute-done.8.refs_2_, bf16[2,64,384]{2,1,0:T(8,128)(2,1)S(1)} %collective-permute-done.9.refs_3_), custom_call_target="tpu_custom_call" | custom-call | tf_op jit(solution)/shard_map/pallas_call | solution.py:233
  (1 shorter events, 0.0 us)
Async XLA Ops:
  0.0 0.7 %copy-start.5 = (bf16[1,1,8,256]{3,2,1,0:T(8,128)(2,1)S(1)}, bf16[1,1,8,256]{3,2,1,0:T(8,128)(2,1)}, u32[]{:S(2)}) copy-start(bf16[1,1,8,256]{3,2,1,0:T(8,128)(2,1)} %param.9) | copy-start | bytes 12292
  0.0 9.5 %collective-permute-start = (bf16[2,128,2048]{2,1,0:T(8,128)(2,1)}, bf16[2,128,2048]{2,1,0:T(8,128)(2,1)S(1)}, u32[]{:S(2)}, u32[]{:S(2)}) collective-permute-start(bf16[2,128,2048]{2,1,0:T(8,128)(2,1)} %bitcast.7), channel_id=1, source_target_pairs={{0,1},{1,0},{2,3},{3,2},{4,5},{5,4},{6,7},{7,6},{8,9},{9,8},{10,11... | collective-permute-start | bytes 3145736 | tf_op jit(solution)/shard_map/ppermute | solution.py:186
  0.7 0.7 %copy-start.4 = (s32[1,1,8,256]{3,2,1,0:T(8,128)S(1)}, s32[1,1,8,256]{3,2,1,0:T(8,128)}, u32[]{:S(2)}) copy-start(s32[1,1,8,256]{3,2,1,0:T(8,128)} %param.8) | copy-start | bytes 24580
  1.4 5.5 %collective-permute-start.1 = (f32[4,256]{1,0:T(4,128)S(1)}, f32[4,256]{1,0:T(4,128)S(1)}, u32[]{:S(2)}, u32[]{:S(2)}) collective-permute-start(f32[4,256]{1,0:T(4,128)S(1)} %get-tuple-element.17), channel_id=1, source_target_pairs={{0,6},{1,7},{2,4},{3,5},{4,2},{5,3},{6,0},{7,1},{8,14},{9,15},{10,... | collective-permute-start | bytes 12296 | tf_op jit(solution)/shard_map/ppermute | solution.py:195
  5.4 0.7 %copy-start.6 = (s32[1,8,4]{1,2,0:T(4,128)S(1)}, s32[1,8,4]{1,2,0:T(4,128)}, u32[]{:S(2)}) copy-start(s32[1,8,4]{1,2,0:T(4,128)} %param.10) | copy-start | bytes 388
  5.4 3.6 %collective-permute-start.2 = (f32[4,256]{1,0:T(4,128)S(1)}, f32[4,256]{1,0:T(4,128)S(1)}, u32[]{:S(2)}, u32[]{:S(2)}) collective-permute-start(f32[4,256]{1,0:T(4,128)S(1)} %get-tuple-element.18), channel_id=1, source_target_pairs={{0,4},{1,5},{2,6},{3,7},{4,0},{5,1},{6,2},{7,3},{8,12},{9,13},{10,... | collective-permute-start | bytes 12296 | tf_op jit(solution)/shard_map/ppermute | solution.py:195
  5.9 3.6 %collective-permute-start.3 = (f32[4,256]{1,0:T(4,128)S(1)}, f32[4,256]{1,0:T(4,128)S(1)}, u32[]{:S(2)}, u32[]{:S(2)}) collective-permute-start(f32[4,256]{1,0:T(4,128)S(1)} %get-tuple-element.19), channel_id=1, source_target_pairs={{0,2},{1,3},{2,0},{3,1},{4,6},{5,7},{6,4},{7,5},{8,10},{9,11},{10,... | collective-permute-start | bytes 12296 | tf_op jit(solution)/shard_map/ppermute | solution.py:195
  6.1 3.4 %copy-start.3 = (s32[1,8,8]{2,1,0:T(8,128)S(1)}, s32[1,8,8]{2,1,0:T(8,128)}, u32[]{:S(2)}) copy-start(s32[1,8,8]{2,1,0:T(8,128)} %param.7) | copy-start | bytes 772
  9.5 1.2 %copy-start = (bf16[2,1,128,2048]{3,2,1,0:T(8,128)(2,1)S(1)}, bf16[2,1,128,2048]{3,2,1,0:T(8,128)(2,1)}, u32[]{:S(2)}) copy-start(bf16[2,1,128,2048]{3,2,1,0:T(8,128)(2,1)} %param.6) | copy-start | bytes 3145732
  10.7 6.7 %copy-start.1 = (bf16[2,1,128,2048]{3,2,1,0:T(8,128)(2,1)S(1)}, bf16[2,1,128,2048]{3,2,1,0:T(8,128)(2,1)}, u32[]{:S(2)}) copy-start(bf16[2,1,128,2048]{3,2,1,0:T(8,128)(2,1)} %param.6) | copy-start | bytes 3145732
  11.9 10.2 %collective-permute-start.4 = (bf16[2,256,256]{2,1,0:T(8,128)(2,1)S(1)}, bf16[2,256,256]{2,1,0:T(8,128)(2,1)S(1)}, u32[]{:S(2)}, u32[]{:S(2)}) collective-permute-start(bf16[2,256,256]{2,1,0:T(8,128)(2,1)S(1)} %get-tuple-element.20), channel_id=1, source_target_pairs={{0,6},{1,7},{2,4},{3,5},{4,2},{5,3},{6,0},{7,1},{8,14},{9,15},{10,... | collective-permute-start | bytes 786440 | tf_op jit(solution)/shard_map/ppermute | solution.py:214
  14.7 10.8 %collective-permute-start.5 = (bf16[2,256,256]{2,1,0:T(8,128)(2,1)S(1)}, bf16[2,256,256]{2,1,0:T(8,128)(2,1)S(1)}, u32[]{:S(2)}, u32[]{:S(2)}) collective-permute-start(bf16[2,256,256]{2,1,0:T(8,128)(2,1)S(1)} %get-tuple-element.21), channel_id=1, source_target_pairs={{0,4},{1,5},{2,6},{3,7},{4,0},{5,1},{6,2},{7,3},{8,12},{9,13},{10,... | collective-permute-start | bytes 786440 | tf_op jit(solution)/shard_map/ppermute | solution.py:214
  16.1 10.5 %collective-permute-start.6 = (bf16[2,256,256]{2,1,0:T(8,128)(2,1)S(1)}, bf16[2,256,256]{2,1,0:T(8,128)(2,1)S(1)}, u32[]{:S(2)}, u32[]{:S(2)}) collective-permute-start(bf16[2,256,256]{2,1,0:T(8,128)(2,1)S(1)} %get-tuple-element.22), channel_id=1, source_target_pairs={{0,2},{1,3},{2,0},{3,1},{4,6},{5,7},{6,4},{7,5},{8,10},{9,11},{10,... | collective-permute-start | bytes 786440 | tf_op jit(solution)/shard_map/ppermute | solution.py:214
  17.5 9.1 %copy-start.2 = (bf16[1,1,8,384,128]{4,3,2,1,0:T(8,128)(2,1)S(1)}, bf16[1,1,8,384,128]{4,3,2,1,0:T(8,128)(2,1)}, u32[]{:S(2)}) copy-start(bf16[1,1,8,384,128]{4,3,2,1,0:T(8,128)(2,1)} %param.11) | copy-start | bytes 2359300
  27.4 7.5 %collective-permute-start.7 = (bf16[2,64,384]{2,1,0:T(8,128)(2,1)S(1)}, bf16[2,64,384]{2,1,0:T(8,128)(2,1)S(1)}, u32[]{:S(2)}, u32[]{:S(2)}) collective-permute-start(bf16[2,64,384]{2,1,0:T(8,128)(2,1)S(1)} %get-tuple-element.24), channel_id=1, source_target_pairs={{0,24},{8,16},{16,8},{24,0},{1,25},{9,17},{17,9},{25,1},{2,26},{10... | collective-permute-start | bytes 294920 | tf_op jit(solution)/shard_map/ppermute | solution.py:231
  30.2 8.3 %collective-permute-start.8 = (bf16[2,64,384]{2,1,0:T(8,128)(2,1)S(1)}, bf16[2,64,384]{2,1,0:T(8,128)(2,1)S(1)}, u32[]{:S(2)}, u32[]{:S(2)}) collective-permute-start(bf16[2,64,384]{2,1,0:T(8,128)(2,1)S(1)} %get-tuple-element.25), channel_id=1, source_target_pairs={{0,16},{8,24},{16,0},{24,8},{1,17},{9,25},{17,1},{25,9},{2,18},{10... | collective-permute-start | bytes 294920 | tf_op jit(solution)/shard_map/ppermute | solution.py:231
  31.3 7.2 %collective-permute-start.9 = (bf16[2,64,384]{2,1,0:T(8,128)(2,1)S(1)}, bf16[2,64,384]{2,1,0:T(8,128)(2,1)S(1)}, u32[]{:S(2)}, u32[]{:S(2)}) collective-permute-start(bf16[2,64,384]{2,1,0:T(8,128)(2,1)S(1)} %get-tuple-element.26), channel_id=1, source_target_pairs={{0,8},{8,0},{16,24},{24,16},{1,9},{9,1},{17,25},{25,17},{2,10},{10... | collective-permute-start | bytes 294920 | tf_op jit(solution)/shard_map/ppermute | solution.py:231

commit v3 on v1

v3 whole, which is shorter than its diff:
```python
import functools

import jax
import jax.numpy as jnp
from jax import lax
from jax.experimental import pallas as pl
from jax.experimental.pallas import tpu as pltpu
from jax.sharding import PartitionSpec as P

TW = 512
LANES = 128
SLAB = TW + LANES
NT_DIMS = (((1,), (1,)), ((), ()))
VMEM = pl.BlockSpec(memory_space=pltpu.VMEM)
HBM = pl.BlockSpec(memory_space=pltpu.HBM)


def target_of(pos, step, count):
    if count & (count - 1) == 0:
        return pos ^ step
    return (pos + step) % count


def source_of(pos, step, count):
    if count & (count - 1) == 0:
        return pos ^ step
    return (pos - step + count) % count


def pairs(step, count):
    return [(pos, target_of(pos, step, count)) for pos in range(count)]


def chip_pairs(step, tiles):
    return [
        (pos, 2 * target_of(pos // 2, step, tiles // 2) + pos % 2) for pos in range(tiles)
    ]


def steps_of(count):
    return list(range(count - 1, 0, -1))


def far_first(count):
    return sorted(range(1, count), key=lambda step: (step.bit_count(), -step))


def chip_of(step, tiles):
    me = lax.axis_index("tile")
    if step == 0:
        return me, me
    chips = tiles // 2
    served = 2 * target_of(me // 2, step, chips) + me % 2
    return served, 2 * source_of(me // 2, step, chips) + me % 2


def wanted_kernel(tiles, index_hbm, frac_hbm, start_hbm, aperture_hbm, traces_hbm, *refs):
    traces_ref, codes_ref, *out_refs, index_ref, frac_ref, start_ref, aperture_ref, sems = refs
    copies = [
        pltpu.make_async_copy(source, target, sems.at[place])
        for place, (source, target) in enumerate(
            [
                (index_hbm, index_ref),
                (frac_hbm, frac_ref),
                (start_hbm, start_ref),
                (aperture_hbm, aperture_ref),
                (traces_hbm, traces_ref),
            ]
        )
    ]
    for copy in copies:
        copy.start()
    for copy in copies[:4]:
        copy.wait()
    me = lax.axis_index("tile")
    rows = index_ref[...].astype(jnp.float32)
    weights = frac_ref[...].astype(jnp.float32)
    starts = start_ref[...]
    slots = aperture_ref[...]
    position = lax.broadcasted_iota(jnp.int32, rows.shape, 0)
    start_tile = lax.broadcasted_iota(jnp.int32, starts.shape, 0)
    start_block = lax.broadcasted_iota(jnp.int32, starts.shape, 1)
    slot_tile = lax.broadcasted_iota(jnp.int32, slots.shape, 1)
    for step, out_ref in enumerate(out_refs):
        tile, block = chip_of(step, tiles)
        for other in range(2):
            mine = position == (block ^ other)
            out_ref[other : other + 1] = jnp.sum(
                jnp.where(mine, rows, 0.0), axis=0, keepdims=True
            )
            out_ref[2 + other : 3 + other] = jnp.sum(
                jnp.where(mine, weights, 0.0), axis=0, keepdims=True
            )
            here = jnp.logical_and(start_tile == tile, start_block == (me ^ other))
            first = jnp.where(here, starts, 0).astype(jnp.float32)
            first = jnp.sum(jnp.sum(first, axis=1, keepdims=True), axis=0, keepdims=True)
            hits = jnp.logical_and(slot_tile == tile, slots == (me ^ other))
            hits = jnp.where(hits, 1.0, 0.0)
            hits = jnp.max(jnp.max(hits, axis=1, keepdims=True), axis=0, keepdims=True)
            code = jnp.where(hits > 0.0, first, -1.0).astype(jnp.int32)
            place = 2 * step + other
            codes_ref[place : place + 1] = jnp.broadcast_to(code, (1, codes_ref.shape[1]))
    copies[4].wait()


def interpolate(columns, other, shift, window):
    row = columns[:, other : other + 1] + shift
    weight = columns[:, 2 + other : 3 + other]
    depth = row.shape[0]
    lane = lax.broadcasted_iota(jnp.int32, (depth, window.shape[1]), 1).astype(jnp.float32)
    hot = jnp.concatenate(
        [(lane == row).astype(jnp.bfloat16), (lane == row + 1.0).astype(jnp.bfloat16)], axis=0
    )
    both = lax.dot_general(hot, window, NT_DIMS, preferred_element_type=jnp.float32)
    return ((1.0 - weight) * both[:depth] + weight * both[depth:]).astype(jnp.bfloat16)


def depth_kernel(step, codes_ref, own_ref, other_ref, wanted_ref, out_ref):
    last = own_ref.shape[2] // LANES - SLAB // LANES
    columns = wanted_ref[...].T
    for other, traces_ref in enumerate((own_ref, other_ref)):
        first = codes_ref[2 * step + other, 0]

        @pl.when(first >= 0)
        def _():
            slab = pl.multiple_of(jnp.minimum(first // LANES, last) * LANES, LANES)
            window = jnp.concatenate(
                [traces_ref[0, :, pl.ds(slab, SLAB)], traces_ref[1, :, pl.ds(slab, SLAB)]], axis=0
            )
            shift = (first - slab).astype(jnp.float32)
            out_ref[other] = interpolate(columns, other, shift, window)

        @pl.when(first < 0)
        def _():
            out_ref[other] = jnp.zeros(out_ref.shape[1:], out_ref.dtype)


def partial_kernel(tiles, shots, steps, amplitude_ref, *refs):
    my_shot = lax.axis_index("shot")
    depth_refs = refs[: len(steps)]
    own_ref, out_refs, total_ref = refs[len(steps)], refs[len(steps) + 1 : -1], refs[-1]
    receivers = amplitude_ref.shape[2]
    span = own_ref.shape[1]
    group = 4
    for base in range(0, len(steps), group):
        places = range(base, min(base + group, len(steps)))
        weights = []
        for place in places:
            _, block = chip_of(steps[place], tiles)
            weights += [amplitude_ref[block], amplitude_ref[block ^ 1]]
        weights = jnp.concatenate(weights, axis=1)
        for part in range(2):
            lanes = slice(part * receivers, (part + 1) * receivers)
            traces = jnp.concatenate(
                [depth_refs[place][other, :, lanes] for place in places for other in range(2)],
                axis=1,
            )
            added = lax.dot_general(traces, weights, NT_DIMS, preferred_element_type=jnp.float32)
            if base:
                added = added + total_ref[part]
            total_ref[part] = added
    for part in range(2):
        own_ref[part] = total_ref[part, pl.ds(pl.multiple_of(my_shot * span, span), span), :]
        for place, step in enumerate(steps_of(shots)):
            target = target_of(my_shot, step, shots)
            rows = pl.ds(pl.multiple_of(target * span, span), span)
            out_refs[place][part] = total_ref[part, rows, :].astype(jnp.bfloat16)


def image_kernel(shots, *refs):
    out_ref = refs[-1]
    stack = None
    for ref in refs[:shots]:
        real = ref[0].astype(jnp.float32)
        imag = ref[1].astype(jnp.float32)
        inverse = 1.0 / jnp.maximum(jnp.sqrt(real * real + imag * imag), 1.0)
        if stack is None:
            stack, first, second = real, real * inverse, imag * inverse
        else:
            stack = stack + real
            first = first + real * inverse
            second = second + imag * inverse
    out_ref[...] = stack * (first * first + second * second) / (shots * shots)


def local(traces, start, depth_index, depth_frac, aperture, amplitude):
    tiles = lax.axis_size("tile")
    shots = lax.axis_size("shot")
    parts, _, receivers, samples = traces.shape
    depth = depth_index.shape[3]
    columns = amplitude.shape[3]
    piece = depth // shots
    chips = tiles // 2
    away = far_first(chips)
    params = pltpu.CompilerParams(vmem_limit_bytes=32 << 20)
    small = pltpu.CompilerParams(vmem_limit_bytes=8 << 20)

    other_traces = lax.ppermute(traces[:, 0], "tile", [(pos, pos ^ 1) for pos in range(tiles)])

    inputs = [depth_index[0, 0], depth_frac[0, 0], start[0], aperture[0].T, traces[:, 0]]
    own_traces, codes, *wanted = pl.pallas_call(
        functools.partial(wanted_kernel, tiles),
        out_shape=[
            jax.ShapeDtypeStruct((parts, receivers, samples), traces.dtype),
            jax.ShapeDtypeStruct((tiles, LANES), jnp.int32),
        ]
        + [jax.ShapeDtypeStruct((4, depth), jnp.float32)] * chips,
        in_specs=[HBM] * len(inputs),
        out_specs=[VMEM] * (2 + chips),
        scratch_shapes=[pltpu.VMEM(value.shape, value.dtype) for value in inputs[:-1]]
        + [pltpu.SemaphoreType.DMA((len(inputs),))],
        compiler_params=params,
    )(*[pltpu.with_memory_space_constraint(value, pltpu.HBM) for value in inputs])
    asked = {
        step: lax.ppermute(wanted[step], "tile", chip_pairs(step, tiles))
        for step in away
    }

    def depth_traces(step, request):
        return pl.pallas_call(
            functools.partial(depth_kernel, step),
            out_shape=jax.ShapeDtypeStruct((2, depth, parts * receivers), jnp.bfloat16),
            in_specs=[VMEM] * 4,
            out_specs=VMEM,
            compiler_params=params,
            cost_estimate=pl.CostEstimate(
                flops=8 * depth * SLAB * parts * receivers,
                bytes_accessed=8 * parts * receivers * (samples + depth),
                transcendentals=0,
            ),
        )(codes, own_traces, other_traces, request)

    kept = depth_traces(0, wanted[0])
    received = [kept]
    for step in away:
        request = asked[step]
        sent = depth_traces(step, request)
        received.append(lax.ppermute(sent, "tile", chip_pairs(step, tiles)))

    own = jax.ShapeDtypeStruct((parts, piece, columns), jnp.float32)
    other = jax.ShapeDtypeStruct((parts, piece, columns), jnp.bfloat16)
    pieces = pl.pallas_call(
        functools.partial(partial_kernel, tiles, shots, [0] + away),
        out_shape=[own] + [other] * (shots - 1),
        in_specs=[VMEM] * (1 + chips),
        out_specs=[VMEM] * shots,
        scratch_shapes=[pltpu.VMEM((parts, depth, columns), jnp.float32)],
        compiler_params=params,
    )(amplitude[0, 0], *received)
    summed = [pieces[0]]
    for place, step in enumerate(steps_of(shots)):
        summed.append(lax.ppermute(pieces[1 + place], "shot", pairs(step, shots)))

    image = pl.pallas_call(
        functools.partial(image_kernel, shots),
        out_shape=jax.ShapeDtypeStruct((piece, columns), jnp.float32),
        in_specs=[VMEM] * shots,
        out_specs=VMEM,
        compiler_params=small,
    )(*summed)
    return image.T


def solution(mesh):
    in_specs = (
        P(None, "shot", "tile", None),
        P("shot", None, None),
        P("shot", "tile", None, None),
        P("shot", "tile", None, None),
        P("shot", None, None),
        P("shot", "tile", None, None, None),
    )
    out_specs = P("tile", "shot")
    return jax.shard_map(local, mesh=mesh, in_specs=in_specs, out_specs=out_specs, check_vma=False)
```

time: 49.2 us -> 36.1 us (0.73)
  starting transfers between devices: 16.1 us -> 11.5 us
  local copies, waits for them, and re-layouts: 4.04 us -> 0.01 us
  waiting for transfers between devices: 22.6 us -> 18.8 us
  other arithmetic: 1.33 us -> 0 us
  Pallas kernels: 5 us -> 5.85 us
    all_to_all x1 -> x0, starting transfers between devices: 5.3 us -> none  [local(): lax.all_to_all(wanted, 'tile', split_axis=0, concat_axis=0, tiled=True)]
    all_to_all x1 -> x0, waiting for transfers between devices: 4.67 us -> none  [local(): lax.all_to_all(wanted, 'tile', split_axis=0, concat_axis=0, tiled=True)]
    unnamed x19 -> x2, local copies, waits for them, and re-layouts: 3.94 us -> 0.01 us
    pallas_call x2 -> x6, Pallas kernels: 3.02 us -> 4.95 us  [the longest x4 2.85 us: depth_traces(): pl.pallas_call(functools.partial(depth_kernel, step), out_shape=jax.Shape...]
    pallas_call x1, Pallas kernels: 1.98 us -> 0.9 us  [local(): pl.pallas_call(functools.partial(image_kernel, shots), out_shape=jax.Shap...]
    ppermute x10, waiting for transfers between devices: 17.9 us -> 18.8 us  [the longest x3 11.3 us: local(): received.append(lax.ppermute(sent, 'tile', chip_pairs(step, tiles)))]
    ppermute x10, starting transfers between devices: 10.8 us -> 11.5 us  [the longest x3 4.45 us: local(): summed.append(lax.ppermute(pieces[1 + place], 'shot', pairs(step, shots)))]
    convert_element_type x2 -> x0, other arithmetic: 0.71 us -> none  [the longest x1 0.7 us: local(): depth_index[0, 0].astype(jnp.float32)]
  transfers between devices with their start and end apart: 11 -> 10, of which waited for: 6 -> 6; matrix products, arithmetic and copies ran while one was open for 0% -> 0% of each run, Pallas kernels for 0% -> 12%
where the time goes in v3:
time: 36.1 us; the launch traced here: 36.3 us
  waiting for transfers between devices  18.8 us (52%)
  starting transfers between devices  11.5 us (32%)
  Pallas kernels  5.85 us (16%)
    ppermute x3, waiting for transfers between devices, local(): received.append(lax.ppermute(sent, 'tile', chip_pairs(step, tiles)))  11.3 us
    ppermute x3, waiting for transfers between devices, local(): summed.append(lax.ppermute(pieces[1 + place], 'shot', pairs(step, shots)))  7.04 us
    ppermute x3, starting transfers between devices, local(): summed.append(lax.ppermute(pieces[1 + place], 'shot', pairs(step, shots)))  4.45 us
    ppermute x3, starting transfers between devices, local(): lax.ppermute(wanted[step], 'tile', chip_pairs(step, tiles))  4.12 us
    pallas_call x4, Pallas kernels, depth_traces(): pl.pallas_call(functools.partial(depth_kernel, step), out_shape=jax.Shape...  2.85 us
    ppermute x3, starting transfers between devices, local(): received.append(lax.ppermute(sent, 'tile', chip_pairs(step, tiles)))  2.47 us
    pallas_call x1, Pallas kernels, local(): pl.pallas_call(functools.partial(wanted_kernel, tiles), out_shape=[jax.Sh...  1.33 us
    pallas_call x1, Pallas kernels, local(): pl.pallas_call(functools.partial(image_kernel, shots), out_shape=jax.Shap...  0.9 us
  transfers between devices with their start and end apart: 10, of which 6 were waited for; matrix products, arithmetic and copies ran while one was open for 0% of the time, Pallas kernels for 12%

profile of v3, /device:TPU:0, one launch (start us, length us, event | category | flops | bytes accessed | tf_op | source)
XLA Modules:
  0.0 36.3 jit_solution(12140722959023050250)
XLA Ops:
  0.0 0.5 %collective-permute-start = (bf16[2,128,2048]{2,1,0:T(8,128)(2,1)}, bf16[2,128,2048]{2,1,0:T(8,128)(2,1)S(1)}, u32[]{:S(2)}, u32[]{:S(2)}) collective-permute-start(bf16[2,128,2048]{2,1,0:T(8,128)(2,1)} %bitcast.10), channel_id=1, source_target_pairs={{0,1},{1,0},{2,3},{3,2},{4,5},{5,4},{6,7},{7,6},{8,9},{9,8},{10,11... | collective-permute-start | bytes 3145736 | tf_op jit(solution)/shard_map/ppermute | solution.py:198
  0.5 1.3 %shard_map.64 = (bf16[2,128,2048]{2,1,0:T(8,128)(2,1)S(1)}, s32[8,128]{1,0:T(8,128)S(1)}, f32[4,256]{1,0:T(4,128)S(1)}, f32[4,256]{1,0:T(4,128)S(1)}, f32[4,256]{1,0:T(4,128)S(1)}, /*index=5*/f32[4,256]{1,0:T(4,128)S(1)}) custom-call(s32[8,256]{1,0:T(8,128)} %bitcast.12, bf16[8,256]{1,0:T(8,128)(2,1)} %bitcast.13, s32[8,8]{1,0:T(8,128)} %bitcast.14, ...), custom_call_target="tpu_custom_call" | custom-call | tf_op jit(solution)/shard_map/pallas_call | solution.py:201
  1.8 2.6 %collective-permute-start.1 = (f32[4,256]{1,0:T(4,128)S(1)}, f32[4,256]{1,0:T(4,128)S(1)}, u32[]{:S(2)}, u32[]{:S(2)}) collective-permute-start(f32[4,256]{1,0:T(4,128)S(1)} %get-tuple-element.18), channel_id=1, source_target_pairs={{0,4},{1,5},{2,6},{3,7},{4,0},{5,1},{6,2},{7,3},{8,12},{9,13},{10,... | collective-permute-start | bytes 12296 | tf_op jit(solution)/shard_map/ppermute | solution.py:215
  4.4 1.5 %collective-permute-start.3 = (f32[4,256]{1,0:T(4,128)S(1)}, f32[4,256]{1,0:T(4,128)S(1)}, u32[]{:S(2)}, u32[]{:S(2)}) collective-permute-start(f32[4,256]{1,0:T(4,128)S(1)} %get-tuple-element.19), channel_id=1, source_target_pairs={{0,2},{1,3},{2,0},{3,1},{4,6},{5,7},{6,4},{7,5},{8,10},{9,11},{10,... | collective-permute-start | bytes 12296 | tf_op jit(solution)/shard_map/ppermute | solution.py:215
  5.9 0.0 collective-permute-start.5
  5.9 0.0 collective-permute-done.1.wanted_ref
  6.0 0.0 collective-permute-done.other_ref
  6.0 1.0 %shard_map.66 = bf16[2,256,256]{2,1,0:T(8,128)(2,1)S(1)} custom-call(s32[8,128]{1,0:T(8,128)S(1)} %get-tuple-element.15.codes_ref, bf16[2,128,2048]{2,1,0:T(8,128)(2,1)S(1)} %get-tuple-element.16.own_ref, bf16[2,128,2048]{2,1,0:T(8,128)(2,1)S(1)} %collective-permute-done.other_ref, f32[4,256]{1,0:T(4,128)S(1)} %collective-permute-done.1.wanted_ref), custom_call_target="tpu_custom_call" | custom-call | flops 335544320 | bytes 4718592 | tf_op jit(solution)/shard_map/pallas_call | solution.py:220
  7.0 1.7 %collective-permute-start.2 = (bf16[2,256,256]{2,1,0:T(8,128)(2,1)S(1)}, bf16[2,256,256]{2,1,0:T(8,128)(2,1)S(1)}, u32[]{:S(2)}, u32[]{:S(2)}) collective-permute-start(bf16[2,256,256]{2,1,0:T(8,128)(2,1)S(1)} %shard_map.66), channel_id=1, source_target_pairs={{0,4},{1,5},{2,6},{3,7},{4,0},{5,1},{6,2},{7,3},{8,12},{9,13},{10,... | collective-permute-start | bytes 786440 | tf_op jit(solution)/shard_map/ppermute | solution.py:238
  8.7 0.0 collective-permute-done.3.wanted_ref
  8.7 0.6 %shard_map.67 = bf16[2,256,256]{2,1,0:T(8,128)(2,1)S(1)} custom-call(s32[8,128]{1,0:T(8,128)S(1)} %get-tuple-element.15.codes_ref, bf16[2,128,2048]{2,1,0:T(8,128)(2,1)S(1)} %get-tuple-element.16.own_ref, bf16[2,128,2048]{2,1,0:T(8,128)(2,1)S(1)} %collective-permute-done.other_ref, f32[4,256]{1,0:T(4,128)S(1)} %collective-permute-done.3.wanted_ref), custom_call_target="tpu_custom_call" | custom-call | flops 335544320 | bytes 4718592 | tf_op jit(solution)/shard_map/pallas_call | solution.py:220
  9.3 0.7 %collective-permute-start.4 = (bf16[2,256,256]{2,1,0:T(8,128)(2,1)S(1)}, bf16[2,256,256]{2,1,0:T(8,128)(2,1)S(1)}, u32[]{:S(2)}, u32[]{:S(2)}) collective-permute-start(bf16[2,256,256]{2,1,0:T(8,128)(2,1)S(1)} %shard_map.67), channel_id=1, source_target_pairs={{0,2},{1,3},{2,0},{3,1},{4,6},{5,7},{6,4},{7,5},{8,10},{9,11},{10,... | collective-permute-start | bytes 786440 | tf_op jit(solution)/shard_map/ppermute | solution.py:238
  10.0 0.5 %collective-permute-done.5.wanted_ref = f32[4,256]{1,0:T(4,128)S(1)} collective-permute-done((f32[4,256]{1,0:T(4,128)S(1)}, f32[4,256]{1,0:T(4,128)S(1)}, u32[]{:S(2)}, u32[]{:S(2)}) %collective-permute-start.5) | collective-permute-done | bytes 4128 | tf_op jit(solution)/shard_map/ppermute | solution.py:215
  10.5 1.0 %shard_map.68 = bf16[2,256,256]{2,1,0:T(8,128)(2,1)S(1)} custom-call(s32[8,128]{1,0:T(8,128)S(1)} %get-tuple-element.15.codes_ref, bf16[2,128,2048]{2,1,0:T(8,128)(2,1)S(1)} %get-tuple-element.16.own_ref, bf16[2,128,2048]{2,1,0:T(8,128)(2,1)S(1)} %collective-permute-done.other_ref, f32[4,256]{1,0:T(4,128)S(1)} %collective-permute-done.5.wanted_ref), custom_call_target="tpu_custom_call" | custom-call | flops 335544320 | bytes 4718592 | tf_op jit(solution)/shard_map/pallas_call | solution.py:220
  11.5 0.1 collective-permute-start.6
  11.6 0.0 copy-start
  11.6 0.2 shard_map.65.refs_0_
  11.8 3.4 %collective-permute-done.2.refs_1_ = bf16[2,256,256]{2,1,0:T(8,128)(2,1)S(1)} collective-permute-done((bf16[2,256,256]{2,1,0:T(8,128)(2,1)S(1)}, bf16[2,256,256]{2,1,0:T(8,128)(2,1)S(1)}, u32[]{:S(2)}, u32[]{:S(2)}) %collective-permute-start.2) | collective-permute-done | bytes 262176 | tf_op jit(solution)/shard_map/ppermute | solution.py:238
  15.2 3.4 %collective-permute-done.4.refs_2_ = bf16[2,256,256]{2,1,0:T(8,128)(2,1)S(1)} collective-permute-done((bf16[2,256,256]{2,1,0:T(8,128)(2,1)S(1)}, bf16[2,256,256]{2,1,0:T(8,128)(2,1)S(1)}, u32[]{:S(2)}, u32[]{:S(2)}) %collective-permute-start.4) | collective-permute-done | bytes 262176 | tf_op jit(solution)/shard_map/ppermute | solution.py:238
  18.6 4.5 %collective-permute-done.6.refs_3_ = bf16[2,256,256]{2,1,0:T(8,128)(2,1)S(1)} collective-permute-done((bf16[2,256,256]{2,1,0:T(8,128)(2,1)S(1)}, bf16[2,256,256]{2,1,0:T(8,128)(2,1)S(1)}, u32[]{:S(2)}, u32[]{:S(2)}) %collective-permute-start.6) | collective-permute-done | bytes 262176 | tf_op jit(solution)/shard_map/ppermute | solution.py:238
  23.1 0.0 copy-done
  23.1 0.8 %shard_map.69 = (f32[2,64,384]{2,1,0:T(8,128)S(1)}, bf16[2,64,384]{2,1,0:T(8,128)(2,1)S(1)}, bf16[2,64,384]{2,1,0:T(8,128)(2,1)S(1)}, bf16[2,64,384]{2,1,0:T(8,128)(2,1)S(1)}) custom-call(bf16[8,384,128]{2,1,0:T(8,128)(2,1)S(1)} %bitcast.9, bf16[2,256,256]{2,1,0:T(8,128)(2,1)S(1)} %shard_map.65.refs_0_, ...), custom_call_target="tpu_custom_call" | custom-call | tf_op jit(solution)/shard_map/pallas_call | solution.py:242
  23.9 2.8 %collective-permute-start.7 = (bf16[2,64,384]{2,1,0:T(8,128)(2,1)S(1)}, bf16[2,64,384]{2,1,0:T(8,128)(2,1)S(1)}, u32[]{:S(2)}, u32[]{:S(2)}) collective-permute-start(bf16[2,64,384]{2,1,0:T(8,128)(2,1)S(1)} %get-tuple-element.22), channel_id=1, source_target_pairs={{0,24},{8,16},{16,8},{24,0},{1,25},{9,17},{17,9},{25,1},{2,26},{10... | collective-permute-start | bytes 294920 | tf_op jit(solution)/shard_map/ppermute | solution.py:252
  26.7 0.2 collective-permute-start.8
  26.9 1.4 %collective-permute-start.9 = (bf16[2,64,384]{2,1,0:T(8,128)(2,1)S(1)}, bf16[2,64,384]{2,1,0:T(8,128)(2,1)S(1)}, u32[]{:S(2)}, u32[]{:S(2)}) collective-permute-start(bf16[2,64,384]{2,1,0:T(8,128)(2,1)S(1)} %get-tuple-element.24), channel_id=1, source_target_pairs={{0,8},{8,0},{16,24},{24,16},{1,9},{9,1},{17,25},{25,17},{2,10},{10... | collective-permute-start | bytes 294920 | tf_op jit(solution)/shard_map/ppermute | solution.py:252
  28.3 3.2 %collective-permute-done.7.refs_1_ = bf16[2,64,384]{2,1,0:T(8,128)(2,1)S(1)} collective-permute-done((bf16[2,64,384]{2,1,0:T(8,128)(2,1)S(1)}, bf16[2,64,384]{2,1,0:T(8,128)(2,1)S(1)}, u32[]{:S(2)}, u32[]{:S(2)}) %collective-permute-start.7) | collective-permute-done | bytes 98336 | tf_op jit(solution)/shard_map/ppermute | solution.py:252
  31.5 3.9 %collective-permute-done.8.refs_2_ = bf16[2,64,384]{2,1,0:T(8,128)(2,1)S(1)} collective-permute-done((bf16[2,64,384]{2,1,0:T(8,128)(2,1)S(1)}, bf16[2,64,384]{2,1,0:T(8,128)(2,1)S(1)}, u32[]{:S(2)}, u32[]{:S(2)}) %collective-permute-start.8) | collective-permute-done | bytes 98336 | tf_op jit(solution)/shard_map/ppermute | solution.py:252
  35.4 0.0 collective-permute-done.9.refs_3_
  35.4 0.9 %shard_map.70 = f32[64,384]{1,0:T(8,128)} custom-call(f32[2,64,384]{2,1,0:T(8,128)S(1)} %get-tuple-element.21.refs_0_, bf16[2,64,384]{2,1,0:T(8,128)(2,1)S(1)} %collective-permute-done.7.refs_1_, bf16[2,64,384]{2,1,0:T(8,128)(2,1)S(1)} %collective-permute-done.8.refs_2_, bf16[2,64,384]{2,1,0:T(8,128)(2,1)S(1)} %collective-permute-done.9.refs_3_), custom_call_target="tpu_custom_call" | custom-call | tf_op jit(solution)/shard_map/pallas_call | solution.py:254
Async XLA Ops:
  0.0 6.0 %collective-permute-start = (bf16[2,128,2048]{2,1,0:T(8,128)(2,1)}, bf16[2,128,2048]{2,1,0:T(8,128)(2,1)S(1)}, u32[]{:S(2)}, u32[]{:S(2)}) collective-permute-start(bf16[2,128,2048]{2,1,0:T(8,128)(2,1)} %bitcast.10), channel_id=1, source_target_pairs={{0,1},{1,0},{2,3},{3,2},{4,5},{5,4},{6,7},{7,6},{8,9},{9,8},{10,11... | collective-permute-start | bytes 3145736 | tf_op jit(solution)/shard_map/ppermute | solution.py:198
  1.8 4.2 %collective-permute-start.1 = (f32[4,256]{1,0:T(4,128)S(1)}, f32[4,256]{1,0:T(4,128)S(1)}, u32[]{:S(2)}, u32[]{:S(2)}) collective-permute-start(f32[4,256]{1,0:T(4,128)S(1)} %get-tuple-element.18), channel_id=1, source_target_pairs={{0,4},{1,5},{2,6},{3,7},{4,0},{5,1},{6,2},{7,3},{8,12},{9,13},{10,... | collective-permute-start | bytes 12296 | tf_op jit(solution)/shard_map/ppermute | solution.py:215
  4.4 4.3 %collective-permute-start.3 = (f32[4,256]{1,0:T(4,128)S(1)}, f32[4,256]{1,0:T(4,128)S(1)}, u32[]{:S(2)}, u32[]{:S(2)}) collective-permute-start(f32[4,256]{1,0:T(4,128)S(1)} %get-tuple-element.19), channel_id=1, source_target_pairs={{0,2},{1,3},{2,0},{3,1},{4,6},{5,7},{6,4},{7,5},{8,10},{9,11},{10,... | collective-permute-start | bytes 12296 | tf_op jit(solution)/shard_map/ppermute | solution.py:215
  5.9 4.6 %collective-permute-start.5 = (f32[4,256]{1,0:T(4,128)S(1)}, f32[4,256]{1,0:T(4,128)S(1)}, u32[]{:S(2)}, u32[]{:S(2)}) collective-permute-start(f32[4,256]{1,0:T(4,128)S(1)} %get-tuple-element.20), channel_id=1, source_target_pairs={{0,6},{1,7},{2,4},{3,5},{4,2},{5,3},{6,0},{7,1},{8,14},{9,15},{10,... | collective-permute-start | bytes 12296 | tf_op jit(solution)/shard_map/ppermute | solution.py:215
  7.0 8.2 %collective-permute-start.2 = (bf16[2,256,256]{2,1,0:T(8,128)(2,1)S(1)}, bf16[2,256,256]{2,1,0:T(8,128)(2,1)S(1)}, u32[]{:S(2)}, u32[]{:S(2)}) collective-permute-start(bf16[2,256,256]{2,1,0:T(8,128)(2,1)S(1)} %shard_map.66), channel_id=1, source_target_pairs={{0,4},{1,5},{2,6},{3,7},{4,0},{5,1},{6,2},{7,3},{8,12},{9,13},{10,... | collective-permute-start | bytes 786440 | tf_op jit(solution)/shard_map/ppermute | solution.py:238
  9.3 9.3 %collective-permute-start.4 = (bf16[2,256,256]{2,1,0:T(8,128)(2,1)S(1)}, bf16[2,256,256]{2,1,0:T(8,128)(2,1)S(1)}, u32[]{:S(2)}, u32[]{:S(2)}) collective-permute-start(bf16[2,256,256]{2,1,0:T(8,128)(2,1)S(1)} %shard_map.67), channel_id=1, source_target_pairs={{0,2},{1,3},{2,0},{3,1},{4,6},{5,7},{6,4},{7,5},{8,10},{9,11},{10,... | collective-permute-start | bytes 786440 | tf_op jit(solution)/shard_map/ppermute | solution.py:238
  11.5 11.6 %collective-permute-start.6 = (bf16[2,256,256]{2,1,0:T(8,128)(2,1)S(1)}, bf16[2,256,256]{2,1,0:T(8,128)(2,1)S(1)}, u32[]{:S(2)}, u32[]{:S(2)}) collective-permute-start(bf16[2,256,256]{2,1,0:T(8,128)(2,1)S(1)} %shard_map.68), channel_id=1, source_target_pairs={{0,6},{1,7},{2,4},{3,5},{4,2},{5,3},{6,0},{7,1},{8,14},{9,15},{10,... | collective-permute-start | bytes 786440 | tf_op jit(solution)/shard_map/ppermute | solution.py:238
  11.6 11.5 %copy-start = (bf16[1,1,8,384,128]{4,3,2,1,0:T(8,128)(2,1)S(1)}, bf16[1,1,8,384,128]{4,3,2,1,0:T(8,128)(2,1)}, u32[]{:S(2)}) copy-start(bf16[1,1,8,384,128]{4,3,2,1,0:T(8,128)(2,1)} %param.11) | copy-start | bytes 2359300
  23.9 7.6 %collective-permute-start.7 = (bf16[2,64,384]{2,1,0:T(8,128)(2,1)S(1)}, bf16[2,64,384]{2,1,0:T(8,128)(2,1)S(1)}, u32[]{:S(2)}, u32[]{:S(2)}) collective-permute-start(bf16[2,64,384]{2,1,0:T(8,128)(2,1)S(1)} %get-tuple-element.22), channel_id=1, source_target_pairs={{0,24},{8,16},{16,8},{24,0},{1,25},{9,17},{17,9},{25,1},{2,26},{10... | collective-permute-start | bytes 294920 | tf_op jit(solution)/shard_map/ppermute | solution.py:252
  26.7 8.7 %collective-permute-start.8 = (bf16[2,64,384]{2,1,0:T(8,128)(2,1)S(1)}, bf16[2,64,384]{2,1,0:T(8,128)(2,1)S(1)}, u32[]{:S(2)}, u32[]{:S(2)}) collective-permute-start(bf16[2,64,384]{2,1,0:T(8,128)(2,1)S(1)} %get-tuple-element.23), channel_id=1, source_target_pairs={{0,16},{8,24},{16,0},{24,8},{1,17},{9,25},{17,1},{25,9},{2,18},{10... | collective-permute-start | bytes 294920 | tf_op jit(solution)/shard_map/ppermute | solution.py:252
  26.9 8.5 %collective-permute-start.9 = (bf16[2,64,384]{2,1,0:T(8,128)(2,1)S(1)}, bf16[2,64,384]{2,1,0:T(8,128)(2,1)S(1)}, u32[]{:S(2)}, u32[]{:S(2)}) collective-permute-start(bf16[2,64,384]{2,1,0:T(8,128)(2,1)S(1)} %get-tuple-element.24), channel_id=1, source_target_pairs={{0,8},{8,0},{16,24},{24,16},{1,9},{9,1},{17,25},{25,17},{2,10},{10... | collective-permute-start | bytes 294920 | tf_op jit(solution)/shard_map/ppermute | solution.py:252

commit v4 on v3

--- a/solution.py
+++ b/solution.py
@@ -135,12 +135,8 @@
             out_ref[other] = jnp.zeros(out_ref.shape[1:], out_ref.dtype)
 
 
-def partial_kernel(tiles, shots, steps, amplitude_ref, *refs):
-    my_shot = lax.axis_index("shot")
-    depth_refs = refs[: len(steps)]
-    own_ref, out_refs, total_ref = refs[len(steps)], refs[len(steps) + 1 : -1], refs[-1]
+def add_chips(tiles, steps, amplitude_ref, depth_refs, total_ref, fresh):
     receivers = amplitude_ref.shape[2]
-    span = own_ref.shape[1]
     group = 4
     for base in range(0, len(steps), group):
         places = range(base, min(base + group, len(steps)))
@@ -156,9 +152,22 @@
                 axis=1,
             )
             added = lax.dot_general(traces, weights, NT_DIMS, preferred_element_type=jnp.float32)
-            if base:
+            if base or not fresh:
                 added = added + total_ref[part]
             total_ref[part] = added
+
+
+def gather_kernel(tiles, steps, amplitude_ref, *refs):
+    add_chips(tiles, steps, amplitude_ref, refs[:-1], refs[-1], True)
+
+
+def partial_kernel(tiles, shots, steps, amplitude_ref, before_ref, *refs):
+    my_shot = lax.axis_index("shot")
+    depth_refs = refs[: len(steps)]
+    own_ref, out_refs, total_ref = refs[len(steps)], refs[len(steps) + 1 : -1], refs[-1]
+    span = own_ref.shape[1]
+    total_ref[...] = before_ref[...]
+    add_chips(tiles, steps, amplitude_ref, depth_refs, total_ref, False)
     for part in range(2):
         own_ref[part] = total_ref[part, pl.ds(pl.multiple_of(my_shot * span, span), span), :]
         for place, step in enumerate(steps_of(shots)):
@@ -167,20 +176,26 @@
             out_refs[place][part] = total_ref[part, rows, :].astype(jnp.bfloat16)
 
 
-def image_kernel(shots, *refs):
-    out_ref = refs[-1]
-    stack = None
-    for ref in refs[:shots]:
+def add_shots(refs, sums):
+    stack, first, second = sums
+    for ref in refs:
         real = ref[0].astype(jnp.float32)
         imag = ref[1].astype(jnp.float32)
         inverse = 1.0 / jnp.maximum(jnp.sqrt(real * real + imag * imag), 1.0)
-        if stack is None:
-            stack, first, second = real, real * inverse, imag * inverse
-        else:
-            stack = stack + real
-            first = first + real * inverse
-            second = second + imag * inverse
-    out_ref[...] = stack * (first * first + second * second) / (shots * shots)
+        stack, first, second = stack + real, first + real * inverse, second + imag * inverse
+    return stack, first, second
+
+
+def early_kernel(*refs):
+    zero = jnp.zeros(refs[0].shape[1:], jnp.float32)
+    sums = add_shots(refs[:-1], (zero, zero, zero))
+    for place, value in enumerate(sums):
+        refs[-1][place] = value
+
+
+def image_kernel(shots, sums_ref, *refs):
+    stack, first, second = add_shots(refs[:-1], (sums_ref[0], sums_ref[1], sums_ref[2]))
+    refs[-1][...] = stack * (first * first + second * second) / (shots * shots)
 
 
 def local(traces, start, depth_index, depth_frac, aperture, amplitude):
@@ -239,25 +254,42 @@
 
     own = jax.ShapeDtypeStruct((parts, piece, columns), jnp.float32)
     other = jax.ShapeDtypeStruct((parts, piece, columns), jnp.bfloat16)
+    steps = [0] + away
+    total = jax.ShapeDtypeStruct((parts, depth, columns), jnp.float32)
+    before = pl.pallas_call(
+        functools.partial(gather_kernel, tiles, steps[:-1]),
+        out_shape=total,
+        in_specs=[VMEM] * chips,
+        out_specs=VMEM,
+        compiler_params=params,
+    )(amplitude[0, 0], *received[:-1])
     pieces = pl.pallas_call(
-        functools.partial(partial_kernel, tiles, shots, [0] + away),
+        functools.partial(partial_kernel, tiles, shots, steps[-1:]),
         out_shape=[own] + [other] * (shots - 1),
-        in_specs=[VMEM] * (1 + chips),
+        in_specs=[VMEM] * 3,
         out_specs=[VMEM] * shots,
-        scratch_shapes=[pltpu.VMEM((parts, depth, columns), jnp.float32)],
+        scratch_shapes=[pltpu.VMEM(total.shape, total.dtype)],
         compiler_params=params,
-    )(amplitude[0, 0], *received)
+    )(amplitude[0, 0], before, received[-1])
     summed = [pieces[0]]
     for place, step in enumerate(steps_of(shots)):
         summed.append(lax.ppermute(pieces[1 + place], "shot", pairs(step, shots)))
 
+    early = 2
+    sums = pl.pallas_call(
+        early_kernel,
+        out_shape=jax.ShapeDtypeStruct((3, piece, columns), jnp.float32),
+        in_specs=[VMEM] * early,
+        out_specs=VMEM,
+        compiler_params=params,
+    )(*summed[:early])
     image = pl.pallas_call(
         functools.partial(image_kernel, shots),
         out_shape=jax.ShapeDtypeStruct((piece, columns), jnp.float32),
-        in_specs=[VMEM] * shots,
+        in_specs=[VMEM] * (1 + shots - early),
         out_specs=VMEM,
         compiler_params=small,
-    )(*summed)
+    )(sums, *summed[early:])
     return image.T
 
 

time: 36.1 us -> 35.7 us (0.989); the launches traced: 36.3 us -> 35.4 us
  waiting for transfers between devices: 18.8 us -> 17.4 us
  starting transfers between devices: 11.5 us -> 12.3 us
    ppermute x3, waiting for transfers between devices: 11.3 us -> 9.88 us  [local(): received.append(lax.ppermute(sent, 'tile', chip_pairs(step, tiles)))]
    ppermute x3, starting transfers between devices: 2.47 us -> 3.23 us  [local(): received.append(lax.ppermute(sent, 'tile', chip_pairs(step, tiles)))]
    pallas_call x4, Pallas kernels: 2.85 us -> 2.44 us  [depth_traces(): pl.pallas_call(functools.partial(depth_kernel, step), out_shape=jax.Shape...]
    pallas_call x1 -> x3, Pallas kernels: 0.77 us -> 1.04 us  [the longest x1 0.57 us: local(): pl.pallas_call(functools.partial(gather_kernel, tiles, steps[:-1]), out_s...]
  transfers between devices with their start and end apart: 10 -> 10, of which waited for: 6 -> 6; matrix products, arithmetic and copies ran while one was open for 0% -> 0% of each run, Pallas kernels for 12% -> 13%
where the time goes in v4:
time: 35.7 us; the launch traced here: 35.4 us
  waiting for transfers between devices  17.4 us (49%)
  starting transfers between devices  12.3 us (34%)
  Pallas kernels  5.6 us (16%)
    ppermute x3, waiting for transfers between devices, local(): received.append(lax.ppermute(sent, 'tile', chip_pairs(step, tiles)))  9.88 us
    ppermute x3, waiting for transfers between devices, local(): summed.append(lax.ppermute(pieces[1 + place], 'shot', pairs(step, shots)))  7.03 us
    ppermute x3, starting transfers between devices, local(): summed.append(lax.ppermute(pieces[1 + place], 'shot', pairs(step, shots)))  4.45 us
    ppermute x3, starting transfers between devices, local(): lax.ppermute(wanted[step], 'tile', chip_pairs(step, tiles))  4.12 us
    ppermute x3, starting transfers between devices, local(): received.append(lax.ppermute(sent, 'tile', chip_pairs(step, tiles)))  3.23 us
    pallas_call x4, Pallas kernels, depth_traces(): pl.pallas_call(functools.partial(depth_kernel, step), out_shape=jax.Shape...  2.44 us
    pallas_call x1, Pallas kernels, local(): pl.pallas_call(functools.partial(wanted_kernel, tiles), out_shape=[jax.Sh...  1.33 us
    pallas_call x1, Pallas kernels, local(): pl.pallas_call(functools.partial(image_kernel, shots), out_shape=jax.Shap...  0.79 us
  transfers between devices with their start and end apart: 10, of which 6 were waited for; matrix products, arithmetic and copies ran while one was open for 0% of the time, Pallas kernels for 13%

profile of v4, /device:TPU:0, one launch (start us, length us, event | category | flops | bytes accessed | tf_op | source)
XLA Modules:
  0.0 35.4 jit_solution(9864643652724143231)
XLA Ops:
  0.0 0.5 %collective-permute-start = (bf16[2,128,2048]{2,1,0:T(8,128)(2,1)}, bf16[2,128,2048]{2,1,0:T(8,128)(2,1)S(1)}, u32[]{:S(2)}, u32[]{:S(2)}) collective-permute-start(bf16[2,128,2048]{2,1,0:T(8,128)(2,1)} %bitcast.11), channel_id=1, source_target_pairs={{0,1},{1,0},{2,3},{3,2},{4,5},{5,4},{6,7},{7,6},{8,9},{9,8},{10,11... | collective-permute-start | bytes 3145736 | tf_op jit(solution)/shard_map/ppermute | solution.py:213
  0.5 1.3 %shard_map.64 = (bf16[2,128,2048]{2,1,0:T(8,128)(2,1)S(1)}, s32[8,128]{1,0:T(8,128)S(1)}, f32[4,256]{1,0:T(4,128)S(1)}, f32[4,256]{1,0:T(4,128)S(1)}, f32[4,256]{1,0:T(4,128)S(1)}, /*index=5*/f32[4,256]{1,0:T(4,128)S(1)}) custom-call(s32[8,256]{1,0:T(8,128)} %bitcast.13, bf16[8,256]{1,0:T(8,128)(2,1)} %bitcast.14, s32[8,8]{1,0:T(8,128)} %bitcast.15, ...), custom_call_target="tpu_custom_call" | custom-call | tf_op jit(solution)/shard_map/pallas_call | solution.py:216
  1.8 2.6 %collective-permute-start.1 = (f32[4,256]{1,0:T(4,128)S(1)}, f32[4,256]{1,0:T(4,128)S(1)}, u32[]{:S(2)}, u32[]{:S(2)}) collective-permute-start(f32[4,256]{1,0:T(4,128)S(1)} %get-tuple-element.18), channel_id=1, source_target_pairs={{0,4},{1,5},{2,6},{3,7},{4,0},{5,1},{6,2},{7,3},{8,12},{9,13},{10,... | collective-permute-start | bytes 12296 | tf_op jit(solution)/shard_map/ppermute | solution.py:230
  4.4 1.5 %collective-permute-start.3 = (f32[4,256]{1,0:T(4,128)S(1)}, f32[4,256]{1,0:T(4,128)S(1)}, u32[]{:S(2)}, u32[]{:S(2)}) collective-permute-start(f32[4,256]{1,0:T(4,128)S(1)} %get-tuple-element.19), channel_id=1, source_target_pairs={{0,2},{1,3},{2,0},{3,1},{4,6},{5,7},{6,4},{7,5},{8,10},{9,11},{10,... | collective-permute-start | bytes 12296 | tf_op jit(solution)/shard_map/ppermute | solution.py:230
  5.9 0.0 collective-permute-start.5
  5.9 0.0 collective-permute-done.1.wanted_ref
  6.0 0.0 collective-permute-done.other_ref
  6.0 0.6 %shard_map.66 = bf16[2,256,256]{2,1,0:T(8,128)(2,1)S(1)} custom-call(s32[8,128]{1,0:T(8,128)S(1)} %get-tuple-element.15.codes_ref, bf16[2,128,2048]{2,1,0:T(8,128)(2,1)S(1)} %get-tuple-element.16.own_ref, bf16[2,128,2048]{2,1,0:T(8,128)(2,1)S(1)} %collective-permute-done.other_ref, f32[4,256]{1,0:T(4,128)S(1)} %collective-permute-done.1.wanted_ref), custom_call_target="tpu_custom_call" | custom-call | flops 335544320 | bytes 4718592 | tf_op jit(solution)/shard_map/pallas_call | solution.py:235
  6.6 2.5 %collective-permute-start.2 = (bf16[2,256,256]{2,1,0:T(8,128)(2,1)S(1)}, bf16[2,256,256]{2,1,0:T(8,128)(2,1)S(1)}, u32[]{:S(2)}, u32[]{:S(2)}) collective-permute-start(bf16[2,256,256]{2,1,0:T(8,128)(2,1)S(1)} %shard_map.66), channel_id=1, source_target_pairs={{0,4},{1,5},{2,6},{3,7},{4,0},{5,1},{6,2},{7,3},{8,12},{9,13},{10,... | collective-permute-start | bytes 786440 | tf_op jit(solution)/shard_map/ppermute | solution.py:253
  9.1 0.0 collective-permute-done.3.wanted_ref
  9.1 0.6 %shard_map.67 = bf16[2,256,256]{2,1,0:T(8,128)(2,1)S(1)} custom-call(s32[8,128]{1,0:T(8,128)S(1)} %get-tuple-element.15.codes_ref, bf16[2,128,2048]{2,1,0:T(8,128)(2,1)S(1)} %get-tuple-element.16.own_ref, bf16[2,128,2048]{2,1,0:T(8,128)(2,1)S(1)} %collective-permute-done.other_ref, f32[4,256]{1,0:T(4,128)S(1)} %collective-permute-done.3.wanted_ref), custom_call_target="tpu_custom_call" | custom-call | flops 335544320 | bytes 4718592 | tf_op jit(solution)/shard_map/pallas_call | solution.py:235
  9.7 0.3 collective-permute-start.4
  10.0 0.5 %collective-permute-done.5.wanted_ref = f32[4,256]{1,0:T(4,128)S(1)} collective-permute-done((f32[4,256]{1,0:T(4,128)S(1)}, f32[4,256]{1,0:T(4,128)S(1)}, u32[]{:S(2)}, u32[]{:S(2)}) %collective-permute-start.5) | collective-permute-done | bytes 4128 | tf_op jit(solution)/shard_map/ppermute | solution.py:230
  10.5 1.0 %shard_map.69 = bf16[2,256,256]{2,1,0:T(8,128)(2,1)S(1)} custom-call(s32[8,128]{1,0:T(8,128)S(1)} %get-tuple-element.15.codes_ref, bf16[2,128,2048]{2,1,0:T(8,128)(2,1)S(1)} %get-tuple-element.16.own_ref, bf16[2,128,2048]{2,1,0:T(8,128)(2,1)S(1)} %collective-permute-done.other_ref, f32[4,256]{1,0:T(4,128)S(1)} %collective-permute-done.5.wanted_ref), custom_call_target="tpu_custom_call" | custom-call | flops 335544320 | bytes 4718592 | tf_op jit(solution)/shard_map/pallas_call | solution.py:235
  11.5 0.4 %collective-permute-start.6 = (bf16[2,256,256]{2,1,0:T(8,128)(2,1)S(1)}, bf16[2,256,256]{2,1,0:T(8,128)(2,1)S(1)}, u32[]{:S(2)}, u32[]{:S(2)}) collective-permute-start(bf16[2,256,256]{2,1,0:T(8,128)(2,1)S(1)} %shard_map.69), channel_id=1, source_target_pairs={{0,6},{1,7},{2,4},{3,5},{4,2},{5,3},{6,0},{7,1},{8,14},{9,15},{10,... | collective-permute-start | bytes 786440 | tf_op jit(solution)/shard_map/ppermute | solution.py:253
  11.9 0.0 copy-start
  11.9 0.2 shard_map.65.refs_0_
  12.1 3.0 %collective-permute-done.2.refs_1_ = bf16[2,256,256]{2,1,0:T(8,128)(2,1)S(1)} collective-permute-done((bf16[2,256,256]{2,1,0:T(8,128)(2,1)S(1)}, bf16[2,256,256]{2,1,0:T(8,128)(2,1)S(1)}, u32[]{:S(2)}, u32[]{:S(2)}) %collective-permute-start.2) | collective-permute-done | bytes 262176 | tf_op jit(solution)/shard_map/ppermute | solution.py:253
  15.2 3.8 %collective-permute-done.4.refs_2_ = bf16[2,256,256]{2,1,0:T(8,128)(2,1)S(1)} collective-permute-done((bf16[2,256,256]{2,1,0:T(8,128)(2,1)S(1)}, bf16[2,256,256]{2,1,0:T(8,128)(2,1)S(1)}, u32[]{:S(2)}, u32[]{:S(2)}) %collective-permute-start.4) | collective-permute-done | bytes 262176 | tf_op jit(solution)/shard_map/ppermute | solution.py:253
  19.0 0.0 copy-done
  19.0 0.6 %shard_map.68.before_ref = f32[2,256,384]{2,1,0:T(8,128)S(1)} custom-call(bf16[8,384,128]{2,1,0:T(8,128)(2,1)S(1)} %bitcast.9, bf16[2,256,256]{2,1,0:T(8,128)(2,1)S(1)} %shard_map.65.refs_0_, bf16[2,256,256]{2,1,0:T(8,128)(2,1)S(1)} %collective-permute-done.2.refs_1_, bf16[2,256,256]{2,1,0:T(8,128)(2,1)S(1)} %collective-permute-done.4.refs_2_), custom_call_target="tpu_custom_call" | custom-call | tf_op jit(solution)/shard_map/pallas_call | solution.py:259
  19.6 3.0 %collective-permute-done.6.refs_0_ = bf16[2,256,256]{2,1,0:T(8,128)(2,1)S(1)} collective-permute-done((bf16[2,256,256]{2,1,0:T(8,128)(2,1)S(1)}, bf16[2,256,256]{2,1,0:T(8,128)(2,1)S(1)}, u32[]{:S(2)}, u32[]{:S(2)}) %collective-permute-start.6) | collective-permute-done | bytes 262176 | tf_op jit(solution)/shard_map/ppermute | solution.py:253
  22.6 0.4 %shard_map.70 = (f32[2,64,384]{2,1,0:T(8,128)S(1)}, bf16[2,64,384]{2,1,0:T(8,128)(2,1)S(1)}, bf16[2,64,384]{2,1,0:T(8,128)(2,1)S(1)}, bf16[2,64,384]{2,1,0:T(8,128)(2,1)S(1)}) custom-call(bf16[8,384,128]{2,1,0:T(8,128)(2,1)S(1)} %bitcast.10, f32[2,256,384]{2,1,0:T(8,128)S(1)} %shard_map.68.before_ref, bf16[2,256,256]{2,1,0:T(8,128)(2,1)S(1)} %collective-permute-done.6.refs_0_), custom_call_target="tpu_custom_call" | custom-call | tf_op jit(solution)/shard_map/pallas_call | solution.py:266
  23.0 3.1 %collective-permute-start.7 = (bf16[2,64,384]{2,1,0:T(8,128)(2,1)S(1)}, bf16[2,64,384]{2,1,0:T(8,128)(2,1)S(1)}, u32[]{:S(2)}, u32[]{:S(2)}) collective-permute-start(bf16[2,64,384]{2,1,0:T(8,128)(2,1)S(1)} %get-tuple-element.22), channel_id=1, source_target_pairs={{0,24},{8,16},{16,8},{24,0},{1,25},{9,17},{17,9},{25,1},{2,26},{10... | collective-permute-start | bytes 294920 | tf_op jit(solution)/shard_map/ppermute | solution.py:276
  26.0 0.7 %collective-permute-start.8 = (bf16[2,64,384]{2,1,0:T(8,128)(2,1)S(1)}, bf16[2,64,384]{2,1,0:T(8,128)(2,1)S(1)}, u32[]{:S(2)}, u32[]{:S(2)}) collective-permute-start(bf16[2,64,384]{2,1,0:T(8,128)(2,1)S(1)} %get-tuple-element.23), channel_id=1, source_target_pairs={{0,16},{8,24},{16,0},{24,8},{1,17},{9,25},{17,1},{25,9},{2,18},{10... | collective-permute-start | bytes 294920 | tf_op jit(solution)/shard_map/ppermute | solution.py:276
  26.7 0.7 %collective-permute-start.9 = (bf16[2,64,384]{2,1,0:T(8,128)(2,1)S(1)}, bf16[2,64,384]{2,1,0:T(8,128)(2,1)S(1)}, u32[]{:S(2)}, u32[]{:S(2)}) collective-permute-start(bf16[2,64,384]{2,1,0:T(8,128)(2,1)S(1)} %get-tuple-element.24), channel_id=1, source_target_pairs={{0,8},{8,0},{16,24},{24,16},{1,9},{9,1},{17,25},{25,17},{2,10},{10... | collective-permute-start | bytes 294920 | tf_op jit(solution)/shard_map/ppermute | solution.py:276
  27.4 3.0 %collective-permute-done.7.refs_1_ = bf16[2,64,384]{2,1,0:T(8,128)(2,1)S(1)} collective-permute-done((bf16[2,64,384]{2,1,0:T(8,128)(2,1)S(1)}, bf16[2,64,384]{2,1,0:T(8,128)(2,1)S(1)}, u32[]{:S(2)}, u32[]{:S(2)}) %collective-permute-start.7) | collective-permute-done | bytes 98336 | tf_op jit(solution)/shard_map/ppermute | solution.py:276
  30.4 0.1 shard_map.71.sums_ref
  30.5 4.0 %collective-permute-done.8.refs_0_ = bf16[2,64,384]{2,1,0:T(8,128)(2,1)S(1)} collective-permute-done((bf16[2,64,384]{2,1,0:T(8,128)(2,1)S(1)}, bf16[2,64,384]{2,1,0:T(8,128)(2,1)S(1)}, u32[]{:S(2)}, u32[]{:S(2)}) %collective-permute-start.8) | collective-permute-done | bytes 98336 | tf_op jit(solution)/shard_map/ppermute | solution.py:276
  34.6 0.0 collective-permute-done.9.refs_1_
  34.6 0.8 %shard_map.72 = f32[64,384]{1,0:T(8,128)} custom-call(f32[3,64,384]{2,1,0:T(8,128)S(1)} %shard_map.71.sums_ref, bf16[2,64,384]{2,1,0:T(8,128)(2,1)S(1)} %collective-permute-done.8.refs_0_, bf16[2,64,384]{2,1,0:T(8,128)(2,1)S(1)} %collective-permute-done.9.refs_1_), custom_call_target="tpu_custom_call" | custom-call | tf_op jit(solution)/shard_map/pallas_call | solution.py:286
Async XLA Ops:
  0.0 6.0 %collective-permute-start = (bf16[2,128,2048]{2,1,0:T(8,128)(2,1)}, bf16[2,128,2048]{2,1,0:T(8,128)(2,1)S(1)}, u32[]{:S(2)}, u32[]{:S(2)}) collective-permute-start(bf16[2,128,2048]{2,1,0:T(8,128)(2,1)} %bitcast.11), channel_id=1, source_target_pairs={{0,1},{1,0},{2,3},{3,2},{4,5},{5,4},{6,7},{7,6},{8,9},{9,8},{10,11... | collective-permute-start | bytes 3145736 | tf_op jit(solution)/shard_map/ppermute | solution.py:213
  1.8 4.2 %collective-permute-start.1 = (f32[4,256]{1,0:T(4,128)S(1)}, f32[4,256]{1,0:T(4,128)S(1)}, u32[]{:S(2)}, u32[]{:S(2)}) collective-permute-start(f32[4,256]{1,0:T(4,128)S(1)} %get-tuple-element.18), channel_id=1, source_target_pairs={{0,4},{1,5},{2,6},{3,7},{4,0},{5,1},{6,2},{7,3},{8,12},{9,13},{10,... | collective-permute-start | bytes 12296 | tf_op jit(solution)/shard_map/ppermute | solution.py:230
  4.4 4.7 %collective-permute-start.3 = (f32[4,256]{1,0:T(4,128)S(1)}, f32[4,256]{1,0:T(4,128)S(1)}, u32[]{:S(2)}, u32[]{:S(2)}) collective-permute-start(f32[4,256]{1,0:T(4,128)S(1)} %get-tuple-element.19), channel_id=1, source_target_pairs={{0,2},{1,3},{2,0},{3,1},{4,6},{5,7},{6,4},{7,5},{8,10},{9,11},{10,... | collective-permute-start | bytes 12296 | tf_op jit(solution)/shard_map/ppermute | solution.py:230
  5.9 4.6 %collective-permute-start.5 = (f32[4,256]{1,0:T(4,128)S(1)}, f32[4,256]{1,0:T(4,128)S(1)}, u32[]{:S(2)}, u32[]{:S(2)}) collective-permute-start(f32[4,256]{1,0:T(4,128)S(1)} %get-tuple-element.20), channel_id=1, source_target_pairs={{0,6},{1,7},{2,4},{3,5},{4,2},{5,3},{6,0},{7,1},{8,14},{9,15},{10,... | collective-permute-start | bytes 12296 | tf_op jit(solution)/shard_map/ppermute | solution.py:230
  6.6 8.6 %collective-permute-start.2 = (bf16[2,256,256]{2,1,0:T(8,128)(2,1)S(1)}, bf16[2,256,256]{2,1,0:T(8,128)(2,1)S(1)}, u32[]{:S(2)}, u32[]{:S(2)}) collective-permute-start(bf16[2,256,256]{2,1,0:T(8,128)(2,1)S(1)} %shard_map.66), channel_id=1, source_target_pairs={{0,4},{1,5},{2,6},{3,7},{4,0},{5,1},{6,2},{7,3},{8,12},{9,13},{10,... | collective-permute-start | bytes 786440 | tf_op jit(solution)/shard_map/ppermute | solution.py:253
  9.7 9.3 %collective-permute-start.4 = (bf16[2,256,256]{2,1,0:T(8,128)(2,1)S(1)}, bf16[2,256,256]{2,1,0:T(8,128)(2,1)S(1)}, u32[]{:S(2)}, u32[]{:S(2)}) collective-permute-start(bf16[2,256,256]{2,1,0:T(8,128)(2,1)S(1)} %shard_map.67), channel_id=1, source_target_pairs={{0,2},{1,3},{2,0},{3,1},{4,6},{5,7},{6,4},{7,5},{8,10},{9,11},{10,... | collective-permute-start | bytes 786440 | tf_op jit(solution)/shard_map/ppermute | solution.py:253
  11.5 11.1 %collective-permute-start.6 = (bf16[2,256,256]{2,1,0:T(8,128)(2,1)S(1)}, bf16[2,256,256]{2,1,0:T(8,128)(2,1)S(1)}, u32[]{:S(2)}, u32[]{:S(2)}) collective-permute-start(bf16[2,256,256]{2,1,0:T(8,128)(2,1)S(1)} %shard_map.69), channel_id=1, source_target_pairs={{0,6},{1,7},{2,4},{3,5},{4,2},{5,3},{6,0},{7,1},{8,14},{9,15},{10,... | collective-permute-start | bytes 786440 | tf_op jit(solution)/shard_map/ppermute | solution.py:253
  11.9 7.1 %copy-start = (bf16[1,1,8,384,128]{4,3,2,1,0:T(8,128)(2,1)S(1)}, bf16[1,1,8,384,128]{4,3,2,1,0:T(8,128)(2,1)}, u32[]{:S(2)}) copy-start(bf16[1,1,8,384,128]{4,3,2,1,0:T(8,128)(2,1)} %param.11) | copy-start | bytes 2359300
  23.0 7.5 %collective-permute-start.7 = (bf16[2,64,384]{2,1,0:T(8,128)(2,1)S(1)}, bf16[2,64,384]{2,1,0:T(8,128)(2,1)S(1)}, u32[]{:S(2)}, u32[]{:S(2)}) collective-permute-start(bf16[2,64,384]{2,1,0:T(8,128)(2,1)S(1)} %get-tuple-element.22), channel_id=1, source_target_pairs={{0,24},{8,16},{16,8},{24,0},{1,25},{9,17},{17,9},{25,1},{2,26},{10... | collective-permute-start | bytes 294920 | tf_op jit(solution)/shard_map/ppermute | solution.py:276
  26.0 8.5 %collective-permute-start.8 = (bf16[2,64,384]{2,1,0:T(8,128)(2,1)S(1)}, bf16[2,64,384]{2,1,0:T(8,128)(2,1)S(1)}, u32[]{:S(2)}, u32[]{:S(2)}) collective-permute-start(bf16[2,64,384]{2,1,0:T(8,128)(2,1)S(1)} %get-tuple-element.23), channel_id=1, source_target_pairs={{0,16},{8,24},{16,0},{24,8},{1,17},{9,25},{17,1},{25,9},{2,18},{10... | collective-permute-start | bytes 294920 | tf_op jit(solution)/shard_map/ppermute | solution.py:276
  26.7 7.9 %collective-permute-start.9 = (bf16[2,64,384]{2,1,0:T(8,128)(2,1)S(1)}, bf16[2,64,384]{2,1,0:T(8,128)(2,1)S(1)}, u32[]{:S(2)}, u32[]{:S(2)}) collective-permute-start(bf16[2,64,384]{2,1,0:T(8,128)(2,1)S(1)} %get-tuple-element.24), channel_id=1, source_target_pairs={{0,8},{8,0},{16,24},{24,16},{1,9},{9,1},{17,25},{25,17},{2,10},{10... | collective-permute-start | bytes 294920 | tf_op jit(solution)/shard_map/ppermute | solution.py:276
